TPU v7x, 256 devices: a whole 4x4x8 slice. The times are simulated.
256 devices in a mesh: fsdp: 8 (over x_hi, y), ctx: 32 (over z, x_lo, core).
Axes of the slice: x: 4 (x_hi: 2, x_lo: 2; x = x_hi * 2 + x_lo), y: 4, z: 8, core: 2. Of those that a mesh axis runs over, the one named last changes fastest.
Arguments:
- tokens: bfloat16 [8, 4096, 1024], P('fsdp', 'ctx'), may hold values from -16 to 16
- cotangent: bfloat16 [8, 4096, 1024], P('fsdp', 'ctx'), may hold values from -6 to 6
- w_query: bfloat16 [1024, 512], P('fsdp')
- w_key: bfloat16 [1024, 512], P('fsdp')
- w_value: bfloat16 [1024, 512], P('fsdp'), may hold values from -0.1875 to 0.1875
- w_out: bfloat16 [512, 1024], P('fsdp'), may hold values from -0.25 to 0.25
- block_mask: int32 [32, 32], replicated, may hold values from 0 to 1, as said below
- span_order: int32 [64], replicated, may hold values from 0 to 63, each once
Outputs:
- mixed_out: bfloat16 [8, 4096, 1024], P('fsdp', 'ctx')
- token_grad: bfloat16 [8, 4096, 1024], P('fsdp', 'ctx')
- grad_query: float32 [1024, 512], P(('fsdp', 'ctx'))
- grad_key: float32 [1024, 512], P(('fsdp', 'ctx'))
- grad_value: float32 [1024, 512], P(('fsdp', 'ctx'))
- grad_out: float32 [512, 1024], P(('fsdp', 'ctx'))
Inputs may be any that keep to these rules, and one draw needn't show every extreme that they name: `block_mask`: every diagonal entry is 1.
All inputs are finite; a program needn't handle non-finite values.
Results may differ from a plain program's by a relative error of at most 0.013.
The roundings to bfloat16 on the way count: a program that leaves them out, or rounds other values in their place, can miss the bound.
Values may be sent and summed in bfloat16 or wider, within the bound.
No kernel may reach another device: no remote copies, remote signals or barrier semaphores. Data moves between devices by JAX's collectives and lax.ppermute only.
A program may use at most 128 MiB of HBM per device.

v0:
```python
import math

import jax
import jax.numpy as jnp
from jax import lax
from jax.sharding import PartitionSpec as P

HEADS = 4
HD = 128
BLK = 128
SPAN = 64


NEG = -1e30
HIGH = lax.Precision.HIGHEST


def block_ids(span_order, start, count):
    rows = start + jnp.arange(count, dtype=jnp.int32)
    span = rows // SPAN
    lanes = jnp.arange(span_order.shape[0], dtype=jnp.int32)
    first = jnp.sum(jnp.where(span[:, None] == lanes[None, :], span_order[None, :], 0), axis=1)
    return (first * SPAN + rows % SPAN) // BLK


def allowed_between(mask_f, row_ids, col_ids):
    lanes = jnp.arange(mask_f.shape[0], dtype=jnp.int32)
    left = (row_ids[:, None] == lanes[None, :]).astype(jnp.float32)
    right = (col_ids[:, None] == lanes[None, :]).astype(jnp.float32)
    linked = jnp.dot(jnp.dot(left, mask_f), right.T)
    return linked > 0.5


def over_blocks(step, carry, pieces):
    count = pieces[0].shape[0]
    width = 512
    stacked = tuple((piece.reshape((count // width, width) + piece.shape[1:]) for piece in pieces))

    def scan_step(state, item):
        number, parts = item
        return (step(state, parts, number * width), None)

    numbers = jnp.arange(count // width, dtype=jnp.int32)
    carry, _ = lax.scan(scan_step, carry, (numbers, stacked))
    return carry


def contract_rows(left, right):
    return lax.dot_general(
        left, right, (((0,), (0,)), ((), ())), preferred_element_type=jnp.float32
    )


def contract_cols(left, right):
    return lax.dot_general(
        left, right, (((1,), (1,)), ((), ())), preferred_element_type=jnp.float32
    )


def body(tokens, cotangent, w_query, w_key, w_value, w_out, block_mask, span_order):
    x_rows = tokens[0]
    dy_rows = cotangent[0]
    rows = x_rows.shape[0]
    scale = 1.0 / math.sqrt(HD)
    full_q, full_k, full_v, full_o = (
        lax.all_gather(w_query, "fsdp", axis=0, tiled=True),
        lax.all_gather(w_key, "fsdp", axis=0, tiled=True),
        lax.all_gather(w_value, "fsdp", axis=0, tiled=True),
        lax.all_gather(w_out, "fsdp", axis=0, tiled=True),
    )
    query = jnp.dot(x_rows, full_q, preferred_element_type=jnp.float32).astype(jnp.bfloat16)
    keys = jnp.dot(x_rows, full_k, preferred_element_type=jnp.float32).astype(jnp.bfloat16)
    values = jnp.dot(x_rows, full_v, preferred_element_type=jnp.float32).astype(jnp.bfloat16)
    d_attn = contract_cols(dy_rows, full_o).astype(jnp.bfloat16)
    mask_f = block_mask.astype(jnp.float32)
    own_ids = block_ids(span_order, lax.axis_index("ctx") * rows, rows)
    q_own = query.reshape(rows, HEADS, HD)
    k_own = keys.reshape(rows, HEADS, HD)
    v_own = values.reshape(rows, HEADS, HD)
    g_own = d_attn.reshape(rows, HEADS, HD)

    def sweep_keys(carry, parts, start):
        top, total, out_acc, mix_acc, key_acc, dot_acc = carry
        count = parts[0].shape[0]
        k_part = parts[0].reshape(count, HEADS, HD)
        v_part = parts[1].reshape(count, HEADS, HD)
        keep = allowed_between(mask_f, own_ids, block_ids(span_order, start, count))[None]
        score = (
            jnp.einsum("qhd,khd->hqk", q_own, k_part, preferred_element_type=jnp.float32) * scale
        )
        score = jnp.where(keep, score, NEG)
        new_top = jnp.maximum(top, jnp.max(score, axis=-1))
        fade = jnp.exp(top - new_top)
        prob = jnp.where(keep, jnp.exp(score - new_top[:, :, None]), 0.0)
        k_wide = k_part.astype(jnp.float32)
        v_wide = v_part.astype(jnp.float32)
        total = fade * total + jnp.sum(prob, axis=-1)
        out_acc = fade[:, :, None] * out_acc + jnp.einsum(
            "hqk,khd->hqd", prob, v_wide, precision=HIGH
        )
        d_prob = jnp.einsum("qhd,khd->hqk", g_own, v_part, preferred_element_type=jnp.float32)
        weighted = prob * d_prob
        dot_acc = fade * dot_acc + jnp.sum(weighted, axis=-1)
        mix_acc = fade[:, :, None] * mix_acc + jnp.einsum(
            "hqk,khd->hqd", weighted, k_wide, precision=HIGH
        )
        key_acc = fade[:, :, None] * key_acc + jnp.einsum(
            "hqk,khd->hqd", prob, k_wide, precision=HIGH
        )
        return (new_top, total, out_acc, mix_acc, key_acc, dot_acc)

    flat = jnp.zeros((HEADS, rows), jnp.float32)
    cube = jnp.zeros((HEADS, rows, HD), jnp.float32)
    begin = (jnp.full((HEADS, rows), NEG, jnp.float32), flat, cube, cube, cube, flat)
    top, total, out_acc, mix_acc, key_acc, dot_acc = over_blocks(
        sweep_keys,
        begin,
        (
            lax.all_gather(keys, "ctx", axis=0, tiled=True),
            lax.all_gather(values, "ctx", axis=0, tiled=True),
        ),
    )
    share = 1.0 / total
    combined = out_acc * share[:, :, None]
    log_total = top + jnp.log(total)
    attention = jnp.transpose(combined, (1, 0, 2)).reshape(rows, HEADS * HD).astype(jnp.bfloat16)
    mixed = (
        x_rows.astype(jnp.float32) + jnp.dot(attention, full_o, preferred_element_type=jnp.float32)
    ).astype(jnp.bfloat16)
    delta = dot_acc * share
    log_rows = jnp.transpose(log_total)
    delta_rows = jnp.transpose(delta)

    def key_side(acc, parts, start):
        d_key, d_value = acc
        count = parts[0].shape[0]
        q_part = parts[0].reshape(count, HEADS, HD)
        g_part = parts[1].reshape(count, HEADS, HD)
        lse_part = jnp.transpose(parts[2])
        delta_part = jnp.transpose(parts[3])
        keep = allowed_between(mask_f, block_ids(span_order, start, count), own_ids)[None]
        score = (
            jnp.einsum("khd,qhd->hkq", q_part, k_own, preferred_element_type=jnp.float32) * scale
        )
        score = jnp.where(keep, score, NEG)
        prob = jnp.where(keep, jnp.exp(score - lse_part[:, :, None]), 0.0)
        d_prob = jnp.einsum("khd,qhd->hkq", g_part, v_own, preferred_element_type=jnp.float32)
        d_score = prob * (d_prob - delta_part[:, :, None])
        d_key = d_key + scale * jnp.einsum(
            "hkq,khd->hqd", d_score, q_part.astype(jnp.float32), precision=HIGH
        )
        d_value = d_value + jnp.einsum(
            "hkq,khd->hqd", prob, g_part.astype(jnp.float32), precision=HIGH
        )
        return (d_key, d_value)

    d_query = scale * (mix_acc - delta[:, :, None] * key_acc) * share[:, :, None]
    d_key, d_value = over_blocks(
        key_side,
        (cube, cube),
        (
            lax.all_gather(query.astype(jnp.float32), "ctx", axis=0, tiled=True).astype(
                jnp.bfloat16
            ),
            lax.all_gather(d_attn.astype(jnp.float32), "ctx", axis=0, tiled=True).astype(
                jnp.bfloat16
            ),
            lax.all_gather(log_rows, "ctx", axis=0, tiled=True),
            lax.all_gather(delta_rows, "ctx", axis=0, tiled=True),
        ),
    )

    def to_rows(grad_heads):
        return jnp.transpose(grad_heads, (1, 0, 2)).reshape(rows, HEADS * HD).astype(jnp.bfloat16)

    dq_rows = to_rows(d_query)
    dk_rows = to_rows(d_key)
    dv_rows = to_rows(d_value)
    token_grad = (
        dy_rows.astype(jnp.float32)
        + contract_cols(dq_rows, full_q)
        + contract_cols(dk_rows, full_k)
        + contract_cols(dv_rows, full_v)
    ).astype(jnp.bfloat16)
    grad_q = contract_rows(x_rows, dq_rows)
    grad_k = contract_rows(x_rows, dk_rows)
    grad_v = contract_rows(x_rows, dv_rows)
    grad_o = contract_rows(attention, dy_rows)
    grad_q, grad_k, grad_v, grad_o = (
        lax.psum_scatter(grad_q, ("fsdp", "ctx"), scatter_dimension=0, tiled=True),
        lax.psum_scatter(grad_k, ("fsdp", "ctx"), scatter_dimension=0, tiled=True),
        lax.psum_scatter(grad_v, ("fsdp", "ctx"), scatter_dimension=0, tiled=True),
        lax.psum_scatter(grad_o, ("fsdp", "ctx"), scatter_dimension=0, tiled=True),
    )
    return (mixed[None], token_grad[None], grad_q, grad_k, grad_v, grad_o)


def solution(mesh):
    return jax.shard_map(
        body,
        mesh=mesh,
        in_specs=(
            P("fsdp", "ctx", None),
            P("fsdp", "ctx", None),
            P("fsdp", None),
            P("fsdp", None),
            P("fsdp", None),
            P("fsdp", None),
            P(),
            P(),
        ),
        out_specs=(
            P("fsdp", "ctx", None),
            P("fsdp", "ctx", None),
            P(("fsdp", "ctx"), None),
            P(("fsdp", "ctx"), None),
            P(("fsdp", "ctx"), None),
            P(("fsdp", "ctx"), None),
        ),
        check_vma=False,
    )
```

profile of v0, /device:TPU:1, one launch (start us, length us, event | category | flops | bytes accessed | tf_op | source)
XLA Modules:
  0.0 906.9 jit_solution(11538158528910636079)
XLA Ops:
  10.0 54.4 %all-gather.9.cloned.1.call-done = bf16[1024,512]{1,0:T(8,128)(2,1)} async-done(((bf16[128,512]{1,0:T(8,128)(2,1)}), bf16[1024,512]{1,0:T(8,128)(2,1)}) %all-gather.9.cloned.1.call-update) | async-done | bytes 1048592 | tf_op jit(solution)/shard_map/all_gather | solution.py:67
  64.5 2.3 convolution_convert_fusion.3
  66.8 50.6 %all-gather.15.cloned.1.call-done = bf16[1024,512]{1,0:T(8,128)(2,1)} async-done(((bf16[128,512]{1,0:T(8,128)(2,1)}), bf16[1024,512]{1,0:T(8,128)(2,1)}) %all-gather.15.cloned.1.call-update) | async-done | bytes 1048592 | tf_op jit(solution)/shard_map/all_gather | solution.py:68
  117.4 2.2 convolution_convert_fusion.1
  119.7 50.7 %all-gather.13.cloned.1.call-done = bf16[1024,512]{1,0:T(8,128)(2,1)} async-done(((bf16[128,512]{1,0:T(8,128)(2,1)}), bf16[1024,512]{1,0:T(8,128)(2,1)}) %all-gather.13.cloned.1.call-update) | async-done | bytes 1048592 | tf_op jit(solution)/shard_map/all_gather | solution.py:66
  170.3 2.2 convolution_convert_fusion.2
  176.3 46.9 %all-gather.19.cloned.1.call-done = bf16[512,1024]{1,0:T(8,128)(2,1)} async-done(((bf16[64,1024]{1,0:T(8,128)(2,1)}), bf16[512,1024]{1,0:T(8,128)(2,1)}) %all-gather.19.cloned.1.call-update) | async-done | bytes 1048592 | tf_op jit(solution)/shard_map/all_gather | solution.py:69
  223.1 1.7 convolution_convert_fusion
  225.6 67.4 %all-gather.11.cloned.1.call-done = bf16[4096,512]{1,0:T(8,128)(2,1)} async-done(((bf16[128,512]{1,0:T(8,128)(2,1)}), bf16[4096,512]{1,0:T(8,128)(2,1)}) %all-gather.11.cloned.1.call-update) | async-done | bytes 4194320 | tf_op jit(solution)/shard_map/all_gather | solution.py:119
  292.9 68.8 %all-gather.17.cloned.1.call-done = bf16[4096,512]{1,0:T(8,128)(2,1)} async-done(((bf16[128,512]{1,0:T(8,128)(2,1)}), bf16[4096,512]{1,0:T(8,128)(2,1)}) %all-gather.17.cloned.1.call-update) | async-done | bytes 4194320 | tf_op jit(solution)/shard_map/all_gather | solution.py:120
  362.2 75.1 %while.40 = (s32[]{:T(128)}, f32[4,128]{1,0:T(4,128)S(1)}, f32[4,128]{1,0:T(4,128)S(1)}, f32[4,128,128]{2,1,0:T(8,128)S(1)}, f32[4,128,128]{2,1,0:T(8,128)S(1)},...) while((s32[]{:T(128)}, f32[4,128]{1,0:T(4,128)S(1)}, ...), condition=%wide.region_6.7_spmd.clone, body=%wide.region_1.6_spmd.clone.sunk | while | flops 1351104000 | bytes 16581600 | solution.py:44
  362.2 1.3 constant_dynamic-slice_fusion.10
  371.6 1.3 constant_dynamic-slice_fusion.10
  381.0 1.3 constant_dynamic-slice_fusion.10
  382.7 1.2 dynamic_slice.79
  390.4 1.3 constant_dynamic-slice_fusion.10
  399.8 1.3 constant_dynamic-slice_fusion.10
  401.5 1.2 dynamic_slice.79
  409.2 1.3 constant_dynamic-slice_fusion.10
  418.6 1.3 constant_dynamic-slice_fusion.10
  428.0 1.3 constant_dynamic-slice_fusion.10
  439.9 35.0 %all_gather.37 = f32[4096,4]{0,1:T(4,128)} all-gather(f32[128,4]{0,1:T(4,128)S(1)} %get-tuple-element.758), channel_id=1, replica_groups=mesh['fsdp'=8,'ctx'=32] {'ctx'}, dimensions={0}, use_global_device_ids=true | all-gather | bytes 67584 | tf_op jit(solution)/shard_map/all_gather | solution.py:168
  474.9 33.7 %all_gather.39 = f32[4096,4]{0,1:T(4,128)} all-gather(f32[128,4]{0,1:T(4,128)S(1)} %bitcast.204), channel_id=1, replica_groups=mesh['fsdp'=8,'ctx'=32] {'ctx'}, dimensions={0}, use_global_device_ids=true | all-gather | bytes 67584 | tf_op jit(solution)/shard_map/all_gather | solution.py:169
  509.2 97.2 %while.41 = (s32[]{:T(128)}, f32[4,128,128]{2,1,0:T(8,128)}, f32[4,128,128]{2,1,0:T(8,128)}, s32[8]{0:T(128)}, s32[64]{0:T(128)S(1)}, /*index=5*/bf16[32,32]{1,0...) while((s32[]{:T(128)}, f32[4,128,128]{2,1,0:T(8,128)}, ...), condition=%wide.region_9.10_spmd.clone, body=%wide.region_7.9_spmd.clone.sunk | while | flops 946874368 | bytes 14089224 | solution.py:44
  509.2 1.3 constant_dynamic-slice_fusion.11
  511.4 1.3 dynamic_slice.82
  516.2 1.8 fusion.146
  517.9 1.7 convolution_add_fusion.15
  519.6 1.3 constant_dynamic-slice_fusion.11
  521.9 1.3 dynamic_slice.82
  526.6 2.7 fusion.146
  529.4 2.6 convolution_add_fusion.15
  532.0 1.3 constant_dynamic-slice_fusion.11
  534.3 1.3 dynamic_slice.82
  539.0 2.7 fusion.146
  541.8 2.7 convolution_add_fusion.15
  544.4 1.3 constant_dynamic-slice_fusion.11
  546.7 1.3 dynamic_slice.82
  551.4 2.7 fusion.146
  554.1 2.7 convolution_add_fusion.15
  556.8 1.3 constant_dynamic-slice_fusion.11
  559.1 1.3 dynamic_slice.82
  563.8 2.7 fusion.146
  566.5 2.6 convolution_add_fusion.15
  569.2 1.3 constant_dynamic-slice_fusion.11
  571.5 1.3 dynamic_slice.82
  576.2 2.7 fusion.146
  578.9 2.7 convolution_add_fusion.15
  581.6 1.3 constant_dynamic-slice_fusion.11
  583.8 1.3 dynamic_slice.82
  588.5 2.7 fusion.146
  591.3 2.7 convolution_add_fusion.15
  593.9 1.3 constant_dynamic-slice_fusion.11
  596.2 1.3 dynamic_slice.82
  600.9 2.7 fusion.146
  603.7 2.7 convolution_add_fusion.15
  609.7 1.8 convolution_bitcast_fusion.3
  611.5 1.8 convolution_bitcast_fusion.2
  613.3 1.7 convolution_bitcast_fusion.1
  615.0 1.7 fusion.40
  618.0 1.9 fusion.39
  619.9 1.6 convolution_add_fusion.6
  623.2 270.3 %all-reduce.7.cloned.1.call-done = (f32[1024,512]{0,1:T(8,128)}, f32[1024,512]{0,1:T(8,128)}, f32[1024,512]{0,1:T(8,128)}, f32[512,1024]{1,0:T(8,128)}) async-done(((f32[1024,512]{0,1:T(8,128)}, f32[1024,512]{0,1:T(8,128)}, f32[1024,512]{0,1:T(8,128)}, f32[512,1024]{1,0:T(8,128)}), (f32[1024,512]{0,1:T(8,128)}, f32[1024,512]{0,1:T(8,128)}, f32[1024,512]{0,1:T(8,128)}, ...) | async-done | bytes 8388624
  899.0 1.4 constant_dynamic-slice_fusion.4
  (336 shorter events, 108.7 us)
Async XLA Ops:
  7.2 110.2 %copy-start = (bf16[1,128,1024]{2,1,0:T(8,128)(2,1)S(1)}, bf16[1,128,1024]{2,1,0:T(8,128)(2,1)}, u32[]{:S(2)}) copy-start(bf16[1,128,1024]{2,1,0:T(8,128)(2,1)} %param.12) | copy-start | bytes 786436
  7.2 57.3 %all-gather.9.cloned.1.call-start = ((), (), s32[]{:S(2)}) async-start(), calls=%async_computation | async-start | bytes 1179648 | tf_op jit(solution)/shard_map/all_gather | solution.py:67
  7.9 109.5 %all-gather.15.cloned.1.call-start = ((), (), s32[]{:S(2)}) async-start(), calls=%async_computation.3 | async-start | bytes 1179648 | tf_op jit(solution)/shard_map/all_gather | solution.py:68
  8.7 161.7 %all-gather.13.cloned.1.call-start = ((), (), s32[]{:S(2)}) async-start(), calls=%async_computation.2 | async-start | bytes 1179648 | tf_op jit(solution)/shard_map/all_gather | solution.py:66
  9.4 213.7 %all-gather.19.cloned.1.call-start = ((), (), s32[]{:S(2)}) async-start(), calls=%async_computation.5 | async-start | bytes 1179648 | tf_op jit(solution)/shard_map/all_gather | solution.py:69
  10.0 162.7 %copy-start.19 = (s32[32,32]{1,0:T(8,128)S(1)}, s32[32,32]{1,0:T(8,128)}, u32[]{:S(2)}) copy-start(s32[32,32]{1,0:T(8,128)} %param.18) | copy-start | bytes 12292
  10.0 163.3 %copy-start.16 = (s32[64]{0:T(128)S(1)}, s32[64]{0:T(128)}, u32[]{:S(2)}) copy-start(s32[64]{0:T(128)} %param.19) | copy-start | bytes 772
  10.0 282.9 %all-gather.11.cloned.1.call-start = ((), (), s32[]{:S(2)}) async-start(), calls=%async_computation.1 | async-start | bytes 4325376 | tf_op jit(solution)/shard_map/all_gather | solution.py:119
  66.7 108.1 %copy-start.9 = (bf16[128,512]{1,0:T(8,128)(2,1)S(1)}, bf16[128,512]{1,0:T(8,128)(2,1)}, u32[]{:S(2)}) copy-start(bf16[128,512]{1,0:T(8,128)(2,1)} %convolution_convert_fusion.3) | copy-start | bytes 393220
  66.7 156.4 %copy-start.6 = (bf16[1,128,1024]{2,1,0:T(8,128)(2,1)S(1)}, bf16[1,128,1024]{2,1,0:T(8,128)(2,1)}, u32[]{:S(2)}) copy-start(bf16[1,128,1024]{2,1,0:T(8,128)(2,1)} %param.13) | copy-start | bytes 786436
  66.8 294.9 %all-gather.17.cloned.1.call-start = ((), (), s32[]{:S(2)}) async-start(), calls=%async_computation.4 | async-start | bytes 4325376 | tf_op jit(solution)/shard_map/all_gather | solution.py:120
  119.6 56.0 %copy-start.10 = (bf16[128,512]{1,0:T(8,128)(2,1)S(1)}, bf16[128,512]{1,0:T(8,128)(2,1)}, u32[]{:S(2)}) copy-start(bf16[128,512]{1,0:T(8,128)(2,1)} %convolution_convert_fusion.1) | copy-start | bytes 393220
  119.6 389.0 %all-gather.21.cloned.1.call-start = ((), (), s32[]{:S(2)}) async-start(), calls=%async_computation.6 | async-start | bytes 4325376 | tf_op jit(solution)/shard_map/all_gather | solution.py:162
  172.5 336.0 %all-gather.23.cloned.1.call-start = ((), (), s32[]{:S(2)}) async-start(), calls=%async_computation.7 | async-start | bytes 4325376 | tf_op jit(solution)/shard_map/all_gather | solution.py:165
  224.8 0.7 copy-start.8
  225.5 668.1 %all-reduce.7.cloned.1.call-start = ((), (), s32[]{:S(2)}) async-start(), calls=%async_computation.8 | async-start | bytes 16777216
  439.9 69.3 %copy-start.17 = (f32[4,128]{1,0:T(4,128)}, f32[4,128]{1,0:T(4,128)S(1)}, u32[]{:S(2)}) copy-start(f32[4,128]{1,0:T(4,128)S(1)} %get-tuple-element.746) | copy-start | bytes 6148
  439.9 69.3 %copy-start.18 = (f32[4,128]{1,0:T(4,128)}, f32[4,128]{1,0:T(4,128)S(1)}, u32[]{:S(2)}) copy-start(f32[4,128]{1,0:T(4,128)S(1)} %get-tuple-element.747) | copy-start | bytes 6148
  509.2 5.5 copy-start.15
  510.7 5.0 copy-start.1
  519.6 5.5 copy-start.15
  521.2 5.0 copy-start.1
  532.0 5.5 copy-start.15
  533.6 5.0 copy-start.1
  544.4 5.5 copy-start.15
  545.9 5.0 copy-start.1
  556.8 5.5 copy-start.15
  558.3 5.0 copy-start.1
  569.2 5.5 copy-start.15
  570.7 5.0 copy-start.1
  581.6 5.5 copy-start.15
  583.1 5.0 copy-start.1
  593.9 5.5 copy-start.15
  595.5 5.0 copy-start.1
  608.5 4.9 copy-start.11
  609.7 3.6 copy-start.14
  609.7 5.3 copy-start.13
  611.5 3.5 copy-start.7
  616.8 1.2 copy-start.5
  616.8 3.2 copy-start.4
  616.8 4.7 copy-start.2
  619.9 2.1 copy-start.3
  619.9 2.1 copy-start.12
Sparse Core Ops, SparseCore 0:
  10.7 53.7 all-gather.8
  67.1 50.2 all-gather.14
  120.0 50.2 all-gather.12
  172.8 50.2 all-gather.18
  225.4 67.4 all-gather.10
  295.2 66.4 all-gather.16
  363.5 66.7 all-gather.20
  432.2 66.4 all-gather.22
  616.9 276.6 all-reduce.6
where the time goes:
time: 910 us; the launch traced here: 907 us
  waiting for transfers between devices  612 us (67%)
  matrix products  122 us (13%)
  local copies, waits for them, and re-layouts  71.7 us (8%)
  blocking collectives  68.7 us (8%)
  between operations  14.1 us (2%)
  loops' own time  11.6 us (1%)
    unnamed x10, waiting for transfers between devices  273 us
    all_gather x1, waiting for transfers between devices, body(): lax.all_gather(values, 'ctx', axis=0, tiled=True)  68.8 us
    all_gather x1, waiting for transfers between devices, body(): lax.all_gather(keys, 'ctx', axis=0, tiled=True)  67.4 us
    all_gather x1, waiting for transfers between devices, body(): lax.all_gather(w_key, 'fsdp', axis=0, tiled=True)  54.4 us
    all_gather x1, waiting for transfers between devices, body(): lax.all_gather(w_query, 'fsdp', axis=0, tiled=True)  50.7 us
    all_gather x1, waiting for transfers between devices, body(): lax.all_gather(w_value, 'fsdp', axis=0, tiled=True)  50.6 us
    dynamic_slice x64, local copies, waits for them, and re-layouts, over_blocks(): carry, _ = lax.scan(scan_step, carry, (numbers, stacked))  47.5 us
    all_gather x1, waiting for transfers between devices, body(): lax.all_gather(w_out, 'fsdp', axis=0, tiled=True)  46.9 us
  transfers between devices with their start and end apart: 9, of which 7 were waited for; matrix products, arithmetic and copies ran while one was open for 10% of the time, Pallas kernels for 0%

commit v1 on v0

v1 whole, which is shorter than its diff:
```python
import math

import jax
import jax.numpy as jnp
from jax import lax
from jax.experimental import pallas as pl
from jax.experimental.pallas import tpu as pltpu
from jax.sharding import Mesh
from jax.sharding import PartitionSpec as P

HEADS = 4
HD = 128
SPAN = 64
NF = 8
NZ = 8
ROWS = 512
SUB = 256
NEG = -1e30
SCALE = 1.0 / math.sqrt(HD)
C2 = SCALE * math.log2(math.e)
VMEM_LIMIT = 40 << 20
BF = jnp.bfloat16
F32 = jnp.float32


def dot(a, b):
    return jnp.dot(a, b, preferred_element_type=F32)


def dot_nt(a, b):
    return lax.dot_general(a, b, (((1,), (1,)), ((), ())), preferred_element_type=F32)


def dot_tn(a, b):
    return lax.dot_general(a, b, (((0,), (0,)), ((), ())), preferred_element_type=F32)


def with_bias(s, bias_ref, first):
    parts = [
        s[t * SPAN : (t + 1) * SPAN, :] + bias_ref[first + t] for t in range(s.shape[0] // SPAN)
    ]
    return jnp.concatenate(parts, axis=0)


def fold(s, op):
    return op(s.reshape(s.shape[0] // 8, 8, s.shape[1]), axis=0)


def forward_kernel(q_ref, g_ref, *refs):
    chunks, (bias_ref, o_ref, stat_ref, s_scr, acc, row) = refs[:NZ], refs[NZ:]
    q_t = q_ref[...].T
    g_t = g_ref[...].T
    acc[...] = jnp.zeros_like(acc)
    row[0] = jnp.full_like(row[0], NEG)
    row[1] = jnp.zeros_like(row[1])
    row[2] = jnp.zeros_like(row[2])
    for d in range(NZ):
        kv = chunks[d]

        def find_top(i, top, kv=kv, d=d):
            at = pl.multiple_of(i * SUB, SUB)
            s = dot(kv[pl.ds(at, SUB), :HD], q_t) * C2
            s = with_bias(s, bias_ref, d * 8 + i * (SUB // SPAN))
            s_scr[pl.ds(at, SUB), :] = s
            return jnp.maximum(top, fold(s, jnp.max))

        top = lax.fori_loop(0, ROWS // SUB, find_top, jnp.full((8, ROWS), NEG, F32))
        old = row[0]
        new = jnp.maximum(old, jnp.max(top, axis=0, keepdims=True))
        fade = jnp.exp2(old - new)
        row[0] = new
        acc[...] = acc[...] * fade[0:1]

        def add_up(i, carry, kv=kv, new=new):
            total, mixed = carry
            at = pl.multiple_of(i * SUB, SUB)
            e = jnp.exp2(s_scr[pl.ds(at, SUB), :] - new[0:1])
            v = kv[pl.ds(at, SUB), HD:]
            dp = dot(v, g_t)
            acc[...] += dot(v.T, e.astype(BF))
            return (total + fold(e, jnp.sum), mixed + fold(e * dp, jnp.sum))

        zero = jnp.zeros((8, ROWS), F32)
        total, mixed = lax.fori_loop(0, ROWS // SUB, add_up, (zero, zero))
        row[1] = row[1] * fade + jnp.sum(total, axis=0, keepdims=True)
        row[2] = row[2] * fade + jnp.sum(mixed, axis=0, keepdims=True)
    share = 1.0 / row[1]
    o_ref[...] = (acc[...] * share[0:1]).T.astype(BF)
    stat_ref[0:1, :] = (row[0] + jnp.log2(row[1]))[0:1]
    stat_ref[1:2, :] = (row[2] * share)[0:1]


def query_kernel(q_ref, g_ref, stat_ref, *refs):
    chunks, (bias_ref, dq_ref, acc) = refs[:NZ], refs[NZ:]
    q_t = q_ref[...].T
    g_t = g_ref[...].T
    lse = stat_ref[0:1, :]
    delta = stat_ref[1:2, :]
    acc[...] = jnp.zeros_like(acc)
    for d in range(NZ):
        kv = chunks[d]

        @pl.loop(0, ROWS // SUB)
        def _(i, kv=kv, d=d):
            at = pl.multiple_of(i * SUB, SUB)
            k = kv[pl.ds(at, SUB), :HD]
            s = with_bias(dot(k, q_t) * C2, bias_ref, d * 8 + i * (SUB // SPAN))
            p = jnp.exp2(s - lse)
            dp = dot(kv[pl.ds(at, SUB), HD:], g_t)
            ds = (p * (dp - delta)).astype(BF)
            acc[...] += dot(k.T, ds)

    dq_ref[...] = (acc[...].T * SCALE).astype(BF)


def key_kernel(kv_ref, stat_ref, *refs):
    chunks, (bias_ref, dk_ref, dv_ref, dk_acc, dv_acc) = refs[:NZ], refs[NZ:]
    dk_acc[...] = jnp.zeros_like(dk_acc)
    dv_acc[...] = jnp.zeros_like(dv_acc)
    for d in range(NZ):
        qg = chunks[d]
        q_t = qg[:, :HD].T
        g_t = qg[:, HD:].T
        lse = stat_ref[d, 0:1, :]
        delta = stat_ref[d, 1:2, :]

        @pl.loop(0, ROWS // SUB)
        def _(i, qg=qg, q_t=q_t, g_t=g_t, lse=lse, delta=delta, d=d):
            at = pl.multiple_of(i * SUB, SUB)
            s = dot(kv_ref[pl.ds(at, SUB), :HD], q_t) * C2
            s = with_bias(s, bias_ref, d * 8 + i * (SUB // SPAN))
            p = jnp.exp2(s - lse)
            dp = dot(kv_ref[pl.ds(at, SUB), HD:], g_t)
            ds = (p * (dp - delta)).astype(BF)
            dk_acc[pl.ds(at, SUB), :] += dot(ds, qg[:, :HD])
            dv_acc[pl.ds(at, SUB), :] += dot(p.astype(BF), qg[:, HD:])

    dk_ref[...] = (dk_acc[...] * SCALE).astype(BF)
    dv_ref[...] = dv_acc[...].astype(BF)


def call(kernel, name, out_shape, scratch, flops, *args):
    many = isinstance(out_shape, tuple)
    vmem = pl.BlockSpec(memory_space=pltpu.VMEM)
    return pl.pallas_call(
        kernel,
        name=name,
        out_shape=out_shape,
        in_specs=[vmem] * len(args),
        out_specs=(vmem,) * len(out_shape) if many else vmem,
        scratch_shapes=scratch,
        compiler_params=pltpu.CompilerParams(vmem_limit_bytes=VMEM_LIMIT),
        cost_estimate=pl.CostEstimate(
            flops=flops, bytes_accessed=4 << 20, transcendentals=ROWS * ROWS * NZ
        ),
    )(*args)


def shift(x, axis, size, by):
    return lax.ppermute(x, axis, [((i + by) % size, i) for i in range(size)])


def ring(x):
    out = [None] * NZ
    out[0] = x
    for r in range(1, NZ // 2 + 1):
        out[r] = shift(out[r - 1], "z", NZ, 1)
        if r < NZ // 2:
            out[-r] = shift(out[(-r + 1) % NZ], "z", NZ, -1)
    return out


def spread(x, axis, size):
    many = jnp.broadcast_to(x[None], (size,) + x.shape)
    return lax.all_to_all(many, axis, split_axis=0, concat_axis=0, tiled=True)


def span_bias(block_mask, span_order, z):
    order = jnp.concatenate([span_order, span_order])
    order = lax.dynamic_slice(order, (z * 8,), (64,)) // 2
    hot = (order[:, None] == jnp.arange(32, dtype=jnp.int32)[None, :]).astype(F32)
    linked = dot(dot(hot, block_mask.astype(F32)), hot.T)
    bias = jnp.where(linked > 0.5, 0.0, NEG).astype(F32)
    own_queries = jnp.repeat(bias[:8].T, SPAN, axis=1)
    by_group = jnp.transpose(bias[:, :8].reshape(8, 8, 8), (0, 2, 1))
    own_keys = jnp.repeat(by_group.reshape(64, 8), SPAN, axis=1)
    return own_queries[:, None, :], own_keys[:, None, :]


def body(tokens, cotangent, w_query, w_key, w_value, w_out, block_mask, span_order):
    x_own = tokens[0]
    dy_own = cotangent[0]
    h = lax.axis_index("h")
    z = lax.axis_index("z")
    bias_q, bias_k = span_bias(block_mask, span_order, z)

    def head(w):
        return lax.dynamic_slice(w, (0, h * HD), (w.shape[0], HD))

    w_mine = jnp.concatenate([head(w_query), head(w_key), head(w_value)], axis=1)
    w_head = spread(w_mine, "f", NF).reshape(1024, 3 * HD)
    x = lax.all_gather(x_own, "h", axis=0, tiled=True)
    dy = lax.all_gather(dy_own, "h", axis=0, tiled=True)
    out_full = lax.all_gather(w_out, "f", axis=0, tiled=True)
    out_head = lax.dynamic_slice(out_full, (h * HD, 0), (HD, 1024))

    kv = dot(x, w_head[:, HD:]).astype(BF)
    q = dot(x, w_head[:, :HD]).astype(BF)
    g = dot_nt(dy, out_head).astype(BF)
    kv_all = ring(kv)
    work = 2 * ROWS * ROWS * NZ * HD
    head_rows = jax.ShapeDtypeStruct((ROWS, HD), BF)
    att, stat = call(
        forward_kernel,
        "attn_forward",
        (head_rows, jax.ShapeDtypeStruct((2, ROWS), F32)),
        [
            pltpu.VMEM((ROWS, ROWS), F32),
            pltpu.VMEM((HD, ROWS), F32),
            pltpu.VMEM((3, 8, ROWS), F32),
        ],
        3 * work,
        q,
        g,
        *kv_all,
        bias_q,
    )
    qg_all = ring(jnp.concatenate([q, g], axis=1))
    stats = spread(stat.reshape(1, 8, 128), "z", NZ).reshape(NZ, 2, ROWS)
    stats = lax.dynamic_slice(jnp.concatenate([stats, stats]), (z, 0, 0), (NZ, 2, ROWS))
    dq = call(
        query_kernel,
        "attn_query_side",
        head_rows,
        [pltpu.VMEM((HD, ROWS), F32)],
        3 * work,
        q,
        g,
        stat,
        *kv_all,
        bias_q,
    )
    dk, dv = call(
        key_kernel,
        "attn_key_side",
        (head_rows, head_rows),
        [pltpu.VMEM((ROWS, HD), F32), pltpu.VMEM((ROWS, HD), F32)],
        4 * work,
        kv,
        stats,
        *qg_all,
        bias_k,
    )

    att_all = lax.all_gather(att[None], "h", axis=0, tiled=True)
    att_own = lax.dynamic_slice(att_all, (0, h * 128, 0), (HEADS, 128, HD))
    att_own = jnp.transpose(att_own, (1, 0, 2)).reshape(128, HEADS * HD)
    mixed = (x_own.astype(F32) + dot(att_own, out_full)).astype(BF)

    w_all = lax.all_gather(w_head[None], "h", axis=0, tiled=True)
    d_head = jnp.concatenate([dq, dk, dv], axis=1)
    d_own = lax.all_to_all(
        d_head.reshape(HEADS, 128, 3 * HD), "h", split_axis=0, concat_axis=0, tiled=True
    )
    token_grad = dy_own.astype(F32)
    for i in range(HEADS):
        token_grad = token_grad + dot_nt(d_own[i], w_all[i])
    token_grad = token_grad.astype(BF)

    grad_head = dot_tn(x, d_head).astype(BF).reshape(64, 16 * 3 * HD)
    rows_of = jnp.transpose(att_all, (1, 0, 2)).reshape(ROWS, HEADS * HD)
    grad_out = dot_tn(rows_of, dy).astype(BF).reshape(64, 4, 2 * 1024)
    grad_out = lax.dynamic_slice(grad_out, (0, h, 0), (64, 1, 2048)).reshape(64, 2048)
    terms = jnp.concatenate([grad_head, grad_out], axis=1).reshape(64, 64, 128)
    terms = lax.all_to_all(terms, ("f", "z"), split_axis=0, concat_axis=0, tiled=True)
    summed = jnp.sum(terms.astype(F32), axis=0)
    grad_o = summed[48:].reshape(2, 1024)
    grads = summed[:48].reshape(HEADS, 4, 3 * HD)
    grads = lax.all_to_all(grads, "h", split_axis=0, concat_axis=0, tiled=True)
    grads = jnp.transpose(grads.reshape(HEADS, 4, 3, HD), (2, 1, 0, 3)).reshape(3, 4, HEADS * HD)
    return (mixed[None], token_grad[None], grads[0], grads[1], grads[2], grad_o)


def solution(mesh):
    fine = Mesh(mesh.devices.reshape(NF, NZ, HEADS), ("f", "z", "h"))
    rows = P("f", ("z", "h"), None)
    split = P(("f", "z", "h"), None)
    return jax.shard_map(
        body,
        mesh=fine,
        in_specs=(rows, rows, P("f", None), P("f", None), P("f", None), P("f", None), P(), P()),
        out_specs=(rows, rows, split, split, split, split),
        check_vma=False,
    )
```

time: 910 us -> 283 us (0.31)
  waiting for transfers between devices: 612 us -> 123 us
  matrix products: 122 us -> 14.8 us
  local copies, waits for them, and re-layouts: 71.7 us -> 15.4 us
  starting transfers between devices: 0.36 us -> 46.7 us
  blocking collectives: 68.7 us -> 37.9 us
  Pallas kernels: 0 us -> 28 us
  loops' own time: 11.6 us -> 0 us
    unnamed x10 -> x4, waiting for transfers between devices: 273 us -> 2.07 us
    all_gather x8 -> x4, waiting for transfers between devices: 339 us -> 71.6 us  [the longest x1 53.2 us: body(): out_full = lax.all_gather(w_out, 'f', axis=0, tiled=True)]
    dot_general x100 -> x11, matrix products: 122 us -> 14.8 us  [the longest x5 6.4 us: dot_nt(): lax.dot_general(a, b, (((1,), (1,)), ((), ())), preferred_element_type=F32)]
    all_gather x2 -> x1, blocking collectives: 68.7 us -> 17.8 us  [body(): att_all = lax.all_gather(att[None], 'h', axis=0, tiled=True)]
    dynamic_slice x64 -> x4, local copies, waits for them, and re-layouts: 47.5 us -> 3.5 us  [the longest x1 1.78 us: body(): lax.dynamic_slice(grad_out, (0, h, 0), (64, 1, 2048)).reshape(64, 2048)]
    all_to_all x0 -> x4, waiting for transfers between devices: none -> 33.8 us  [the longest x1 27.1 us: body(): lax.all_to_all(terms, ('f', 'z'), split_axis=0, concat_axis=0, tiled=True)]
    pallas_call x0 -> x3, Pallas kernels: none -> 28 us  [call(): pl.pallas_call(kernel, name=name, out_shape=out_shape, in_specs=[vmem] *...]
    ppermute x0 -> x14, starting transfers between devices: none -> 25.6 us  [shift(): return lax.ppermute(x, axis, [((i + by) % size, i) for i in range(size)])]
  transfers between devices with their start and end apart: 9 -> 22, of which waited for: 7 -> 9; matrix products, arithmetic and copies ran while one was open for 10% -> 10% of each run, Pallas kernels for 0% -> 10%
where the time goes in v1:
time: 283 us; the launch traced here: 282 us
  waiting for transfers between devices  123 us (43%)
  starting transfers between devices  46.7 us (17%)
  blocking collectives  37.9 us (13%)
  Pallas kernels  28 us (10%)
  local copies, waits for them, and re-layouts  15.4 us (5%)
  matrix products  14.8 us (5%)
  between operations  14.1 us (5%)
    all_gather x1, waiting for transfers between devices, body(): out_full = lax.all_gather(w_out, 'f', axis=0, tiled=True)  53.2 us
    pallas_call x3, Pallas kernels, call(): pl.pallas_call(kernel, name=name, out_shape=out_shape, in_specs=[vmem] *...  28 us
    all_to_all x1, waiting for transfers between devices, body(): lax.all_to_all(terms, ('f', 'z'), split_axis=0, concat_axis=0, tiled=True)  27.1 us
    ppermute x14, starting transfers between devices, shift(): return lax.ppermute(x, axis, [((i + by) % size, i) for i in range(size)])  25.6 us
    all_to_all x1, blocking collectives, spread(): return lax.all_to_all(many, axis, split_axis=0, concat_axis=0, tiled=True)  20.1 us
    all_gather x1, blocking collectives, body(): att_all = lax.all_gather(att[None], 'h', axis=0, tiled=True)  17.8 us
    ppermute x14, waiting for transfers between devices, shift(): return lax.ppermute(x, axis, [((i + by) % size, i) for i in range(size)])  15.4 us
    all_gather x1, waiting for transfers between devices, body(): dy = lax.all_gather(dy_own, 'h', axis=0, tiled=True)  11.5 us
  transfers between devices with their start and end apart: 22, of which 9 were waited for; matrix products, arithmetic and copies ran while one was open for 10% of the time, Pallas kernels for 10%

profile of v1, /device:TPU:1, one launch (start us, length us, event | category | flops | bytes accessed | tf_op | source)
XLA Modules:
  0.0 282.2 jit_solution(12033088488977501562)
XLA Ops:
  7.2 0.7 all-gather.12.cloned.1.call-update
  8.0 0.7 all-gather.14.cloned.1.call-update
  8.7 0.7 all-gather.8.cloned.1.call-update
  9.5 0.8 constant_dynamic-slice_fusion.2
  10.4 20.1 %all_to_all.25 = bf16[8,128,384]{2,1,0:T(8,128)(2,1)S(1)} all-to-all(bf16[8,128,384]{2,1,0:T(8,128)(2,1)S(1)} %broadcast_in_dim.38), channel_id=1, replica_groups=mesh['f'=8,'z'=8,'h'=4] {'f'}, dimensions={0} | all-to-all | bytes 1572864 | tf_op jit(solution)/shard_map/all_to_all | solution.py:175
  30.4 6.9 %all-gather.12.cloned.1.call-done = bf16[1,512,1024]{2,1,0:T(8,128)(2,1)} async-done(((bf16[1,128,1024]{2,1,0:T(8,128)(2,1)}), bf16[1,512,1024]{2,1,0:T(8,128)(2,1)}) %all-gather.12.cloned.1.call-update) | async-done | bytes 1048592 | tf_op jit(solution)/shard_map/all_gather | solution.py:202
  37.3 1.7 fusion.3.refs_0_.kv_ref
  39.0 5.2 %collective-permute-start = (bf16[512,256]{1,0:T(8,128)(2,1)S(1)}, bf16[512,256]{1,0:T(8,128)(2,1)S(1)}, u32[]{:S(2)}, u32[]{:S(2)}) collective-permute-start(bf16[512,256]{1,0:T(8,128)(2,1)S(1)} %fusion.3.refs_0_.kv_ref), channel_id=1, source_target_pairs={{4,0},{8,4},{12,8},{16,12},{20,16},{24,20},{28,24},{0,28},{5,1},{9... | collective-permute-start | bytes 786440 | tf_op jit(solution)/shard_map/ppermute | solution.py:160
  44.1 0.1 pad_add_fusion
  44.2 1.7 fusion.7.q_ref
  45.9 4.0 %collective-permute-done.refs_1_ = bf16[512,256]{1,0:T(8,128)(2,1)S(1)} collective-permute-done((bf16[512,256]{1,0:T(8,128)(2,1)S(1)}, bf16[512,256]{1,0:T(8,128)(2,1)S(1)}, u32[]{:S(2)}, u32[]{:S(2)}) %collective-permute-start) | collective-permute-done | bytes 262176 | tf_op jit(solution)/shard_map/ppermute | solution.py:160
  49.9 3.4 %collective-permute-start.1 = (bf16[512,256]{1,0:T(8,128)(2,1)S(1)}, bf16[512,256]{1,0:T(8,128)(2,1)S(1)}, u32[]{:S(2)}, u32[]{:S(2)}) collective-permute-start(bf16[512,256]{1,0:T(8,128)(2,1)S(1)} %collective-permute-done.refs_1_), channel_id=1, source_target_pairs={{4,0},{8,4},{12,8},{16,12},{20,16},{24,20},{28,24},{0,28},{5,1},{9... | collective-permute-start | bytes 786440 | tf_op jit(solution)/shard_map/ppermute | solution.py:160
  53.3 11.5 %all-gather.14.cloned.1.call-done = bf16[1,512,1024]{2,1,0:T(8,128)(2,1)} async-done(((bf16[1,128,1024]{2,1,0:T(8,128)(2,1)}), bf16[1,512,1024]{2,1,0:T(8,128)(2,1)}) %all-gather.14.cloned.1.call-update) | async-done | bytes 1048592 | tf_op jit(solution)/shard_map/all_gather | solution.py:203
  64.9 53.2 %all-gather.8.cloned.1.call-done = bf16[512,1024]{1,0:T(8,128)(2,1)} async-done(((bf16[64,1024]{1,0:T(8,128)(2,1)}), bf16[512,1024]{1,0:T(8,128)(2,1)}) %all-gather.8.cloned.1.call-update) | async-done | bytes 1048592 | tf_op jit(solution)/shard_map/all_gather | solution.py:204
  118.1 1.7 fusion.6.g_ref
  119.9 3.1 %collective-permute-start.7 = (bf16[512,256]{1,0:T(8,128)(2,1)S(1)}, bf16[512,256]{1,0:T(8,128)(2,1)S(1)}, u32[]{:S(2)}, u32[]{:S(2)}) collective-permute-start(bf16[512,256]{1,0:T(8,128)(2,1)S(1)} %pad_maximum_fusion.1.refs_0_), channel_id=1, source_target_pairs={{4,0},{8,4},{12,8},{16,12},{20,16},{24,20},{28,24},{0,28},{5,1},{9... | collective-permute-start | bytes 786440 | tf_op jit(solution)/shard_map/ppermute | solution.py:160
  123.0 2.7 collective-permute-start.2
  125.8 0.1 and_select_fusion
  125.9 0.4 fusion.8
  126.2 9.0 %collective-permute-done.5.refs_6_ = bf16[512,256]{1,0:T(8,128)(2,1)S(1)} collective-permute-done((bf16[512,256]{1,0:T(8,128)(2,1)S(1)}, bf16[512,256]{1,0:T(8,128)(2,1)S(1)}, u32[]{:S(2)}, u32[]{:S(2)}) %collective-permute-start.5) | collective-permute-done | bytes 262176 | tf_op jit(solution)/shard_map/ppermute | solution.py:160
  135.3 2.7 collective-permute-start.8
  138.0 2.7 collective-permute-start.3
  140.6 0.1 copy.31
  140.7 0.1 broadcast_in_dim.41
  140.9 0.2 broadcast_in_dim_reshape.10.refs_8_
  141.1 0.1 copy.41
  141.2 0.1 broadcast_in_dim.46
  141.3 0.2 broadcast_in_dim_reshape.11.refs_8_
  141.5 2.9 %collective-permute-start.9 = (bf16[512,256]{1,0:T(8,128)(2,1)S(1)}, bf16[512,256]{1,0:T(8,128)(2,1)}, u32[]{:S(2)}, u32[]{:S(2)}) collective-permute-start(bf16[512,256]{1,0:T(8,128)(2,1)S(1)} %collective-permute-done.8.refs_2_), channel_id=1, source_target_pairs={{4,0},{8,4},{12,8},{16,12},{20,16},{24,20},{28,24},{0,28},{5,1},{9... | collective-permute-start | bytes 786440 | tf_op jit(solution)/shard_map/ppermute | solution.py:160
  144.4 2.3 collective-permute-done.12.refs_6_
  146.7 9.6 %attn_forward.1 = (bf16[512,128]{1,0:T(8,128)(2,1)S(1)}, f32[2,512]{1,0:T(2,128)S(1)}) custom-call(bf16[512,128]{1,0:T(8,128)(2,1)S(1)} %fusion.7.q_ref, bf16[512,128]{1,0:T(8,128)(2,1)S(1)} %fusion.6.g_ref, bf16[512,256]{1,0:T(8,128)(2,1)S(1)} %fusion.3.refs_0_.kv_ref, bf16[512,256]{1,0:T(8,128)(2,1)S(1)} %collective-permute-done.refs_1_, ...), custom_call_target="tpu_custom_call" | custom-call | flops 1610612736 | bytes 4194304 | tf_op jit(solution)/shard_map/attn_forward/pallas_call | solution.py:145
  156.4 0.6 broadcast_in_dim.45
  157.0 4.2 %all-to-all-start.1 = ((f32[8,1,8,128]{3,2,1,0:T(8,128)}), f32[8,1,8,128]{3,2,1,0:T(8,128)S(1)}, u32[]{:S(2)}, u32[]{:S(2)}) async-start(f32[8,1,8,128]{3,2,1,0:T(8,128)} %broadcast_in_dim.45), calls=%async_computation.1 | async-start | bytes 65536 | tf_op jit(solution)/shard_map/all_to_all | solution.py:175
  161.2 17.8 %all-gather.2 = bf16[2048,128]{1,0:T(8,128)(2,1)} all-gather(bf16[512,128]{1,0:T(8,128)(2,1)S(1)} %get-tuple-element.10), channel_id=4, replica_groups=mesh['f'=8,'z'=8,'h'=4] {'h'}, dimensions={0}, use_global_device_ids=true | all-gather | bytes 655360 | tf_op jit(solution)/shard_map/all_gather | solution.py:255
  179.0 2.1 copy.32
  181.1 3.1 %convolution_convert_fusion = bf16[512,1024]{1,0:T(8,128)(2,1)} fusion(bf16[512,512]{0,1:T(8,128)(2,1)} %bitcast.97, bf16[1,512,1024]{2,1,0:T(8,128)(2,1)} %all-gather.14.cloned.1.call-done), kind=kOutput, calls=%fused_computation.1 | convolution fusion | flops 537395200 | bytes 2621440 | tf_op jit(solution)/shard_map/dot_general | solution.py:35
  184.2 2.6 reshape.74
  186.9 2.9 %collective-permute-start.10 = (bf16[512,256]{1,0:T(8,128)(2,1)}, bf16[512,256]{1,0:T(8,128)(2,1)}, u32[]{:S(2)}, u32[]{:S(2)}) collective-permute-start(bf16[512,256]{1,0:T(8,128)(2,1)} %collective-permute-done.9.refs_3_), channel_id=1, source_target_pairs={{4,0},{8,4},{12,8},{16,12},{20,16},{24,20},{28,24},{0,28},{5,1},{9... | collective-permute-start | bytes 786440 | tf_op jit(solution)/shard_map/ppermute | solution.py:160
  189.8 1.8 constant_dynamic-slice_fusion
  191.6 8.6 %attn_query_side.1 = bf16[512,128]{1,0:T(8,128)(2,1)S(1)} custom-call(bf16[512,128]{1,0:T(8,128)(2,1)S(1)} %fusion.7.q_ref, bf16[512,128]{1,0:T(8,128)(2,1)S(1)} %fusion.6.g_ref, f32[2,512]{1,0:T(2,128)S(1)} %get-tuple-element.11.stat_ref, bf16[512,256]{1,0:T(8,128)(2,1)S(1)} %fusion.3.refs_0_.kv_ref, bf16[512,256]{1,0:T(8,128)(2,1)S(1)} %collective-permute-done.refs_1_, ...), custom_call_target="tpu_custom_call" | custom-call | flops 1610612736 | bytes 4194304 | tf_op jit(solution)/shard_map/attn_query_side/pallas_call | solution.py:145
  200.2 0.9 copy.46
  201.2 9.8 %attn_key_side.1 = (bf16[512,128]{1,0:T(8,128)(2,1)S(1)}, bf16[512,128]{1,0:T(8,128)(2,1)S(1)}) custom-call(bf16[512,256]{1,0:T(8,128)(2,1)S(1)} %fusion.3.refs_0_.kv_ref, f32[8,2,512]{2,1,0:T(2,128)S(1)} %fusion.19.stat_ref, bf16[512,256]{1,0:T(8,128)(2,1)S(1)} %pad_maximum_fusion.1.refs_0_, bf16[512,256]{1,0:T(8,128)(2,1)S(1)} %collective-permute-done.7.refs_1_, ...), custom_call_target="tpu_custom_call" | custom-call | flops 2147483648 | bytes 4194304 | tf_op jit(solution)/shard_map/attn_key_side/pallas_call | solution.py:145
  211.0 0.6 fusion
  211.6 0.4 copy.35
  211.9 1.3 reshape.72
  213.2 1.2 maximum_bitcast_fusion
  214.4 1.3 copy.44
  215.7 6.9 %all-to-all-start.3 = ((bf16[64,64,128]{2,1,0:T(8,128)(2,1)}), bf16[64,64,128]{2,1,0:T(8,128)(2,1)S(1)}, u32[]{:S(2)}, u32[]{:S(2)}) async-start(bf16[64,64,128]{2,1,0:T(8,128)(2,1)} %bitcast.45), calls=%async_computation.3 | async-start | bytes 2097152 | tf_op jit(solution)/shard_map/all_to_all | solution.py:275
  222.6 0.9 constant_dynamic-slice_fusion.1
  223.5 27.1 %all-to-all-done.3 = bf16[64,64,128]{2,1,0:T(8,128)(2,1)S(1)} async-done(((bf16[64,64,128]{2,1,0:T(8,128)(2,1)}), bf16[64,64,128]{2,1,0:T(8,128)(2,1)S(1)}, u32[]{:S(2)}, u32[]{:S(2)}) %all-to-all-start.3) | async-done | bytes 1048608 | tf_op jit(solution)/shard_map/all_to_all | solution.py:275
  250.6 0.2 convert_reduce_fusion
  250.8 0.6 reshape.77
  251.5 5.6 %all-to-all-start.4 = ((f32[4,4,384]{2,1,0:T(4,128)}), f32[4,4,384]{2,1,0:T(4,128)S(1)}, u32[]{:S(2)}, u32[]{:S(2)}) async-start(f32[4,4,384]{2,1,0:T(4,128)} %reshape.77), calls=%async_computation.4 | async-start | bytes 49152 | tf_op jit(solution)/shard_map/all_to_all | solution.py:279
  257.1 0.8 pad_maximum_fusion
  257.9 2.3 all-to-all-done.4
  260.2 4.2 %all-to-all-start.2 = ((bf16[4,128,384]{2,1,0:T(8,128)(2,1)}), bf16[4,128,384]{2,1,0:T(8,128)(2,1)S(1)}, u32[]{:S(2)}, u32[]{:S(2)}) async-start(bf16[4,128,384]{2,1,0:T(8,128)(2,1)} %bitcast.16), calls=%async_computation.2 | async-start | bytes 786432 | tf_op jit(solution)/shard_map/all_to_all | solution.py:262
  264.4 1.0 fusion.4
  265.5 0.6 reshape.79
  266.1 0.6 slice_bitcast_fusion.17
  266.7 4.3 %all-to-all-done.2 = bf16[4,128,384]{2,1,0:T(8,128)(2,1)S(1)} async-done(((bf16[4,128,384]{2,1,0:T(8,128)(2,1)}), bf16[4,128,384]{2,1,0:T(8,128)(2,1)S(1)}, u32[]{:S(2)}, u32[]{:S(2)}) %all-to-all-start.2) | async-done | bytes 393248 | tf_op jit(solution)/shard_map/all_to_all | solution.py:262
  271.0 1.7 convolution_add_fusion.4
  272.7 1.5 convolution_add_fusion.3
  274.2 0.4 convolution_add_fusion.2
  274.6 1.1 fusion.5
  (55 shorter events, 0.5 us)
Async XLA Ops:
  7.2 2.3 copy-start
  7.2 37.0 %copy-start.9 = (s32[64]{0:T(128)S(1)}, s32[64]{0:T(128)}, u32[]{:S(2)}) copy-start(s32[64]{0:T(128)} %param.15) | copy-start | bytes 772
  7.2 30.1 %all-gather.12.cloned.1.call-start = ((), (), s32[]{:S(2)}) async-start(), calls=%async_computation.7 | async-start | bytes 1310720 | tf_op jit(solution)/shard_map/all_gather | solution.py:202
  7.9 57.0 %all-gather.14.cloned.1.call-start = ((), (), s32[]{:S(2)}) async-start(), calls=%async_computation.8 | async-start | bytes 1310720 | tf_op jit(solution)/shard_map/all_gather | solution.py:203
  8.7 109.4 %all-gather.8.cloned.1.call-start = ((), (), s32[]{:S(2)}) async-start(), calls=%async_computation.5 | async-start | bytes 1179648 | tf_op jit(solution)/shard_map/all_gather | solution.py:204
  9.4 261.6 %all-gather.10.cloned.1.call-start = ((), (), s32[]{:S(2)}) async-start(), calls=%async_computation.6 | async-start | bytes 3932160 | tf_op jit(solution)/shard_map/all_gather | solution.py:260
  30.4 34.5 %copy-start.1 = (bf16[8,128,384]{2,1,0:T(8,128)(2,1)}, bf16[8,128,384]{2,1,0:T(8,128)(2,1)S(1)}, u32[]{:S(2)}) copy-start(bf16[8,128,384]{2,1,0:T(8,128)(2,1)S(1)} %all_to_all.25) | copy-start | bytes 2359300
  30.4 95.4 %copy-start.8 = (s32[32,32]{1,0:T(8,128)S(1)}, s32[32,32]{1,0:T(8,128)}, u32[]{:S(2)}) copy-start(s32[32,32]{1,0:T(8,128)} %param.14) | copy-start | bytes 12292
  39.0 11.0 %collective-permute-start = (bf16[512,256]{1,0:T(8,128)(2,1)S(1)}, bf16[512,256]{1,0:T(8,128)(2,1)S(1)}, u32[]{:S(2)}, u32[]{:S(2)}) collective-permute-start(bf16[512,256]{1,0:T(8,128)(2,1)S(1)} %fusion.3.refs_0_.kv_ref), channel_id=1, source_target_pairs={{4,0},{8,4},{12,8},{16,12},{20,16},{24,20},{28,24},{0,28},{5,1},{9... | collective-permute-start | bytes 786440 | tf_op jit(solution)/shard_map/ppermute | solution.py:160
  44.2 78.8 %collective-permute-start.4 = (bf16[512,256]{1,0:T(8,128)(2,1)S(1)}, bf16[512,256]{1,0:T(8,128)(2,1)S(1)}, u32[]{:S(2)}, u32[]{:S(2)}) collective-permute-start(bf16[512,256]{1,0:T(8,128)(2,1)S(1)} %fusion.3.refs_0_.kv_ref), channel_id=1, source_target_pairs={{28,0},{0,4},{4,8},{8,12},{12,16},{16,20},{20,24},{24,28},{29,1},{... | collective-permute-start | bytes 786440 | tf_op jit(solution)/shard_map/ppermute | solution.py:160
  49.9 73.1 %collective-permute-start.1 = (bf16[512,256]{1,0:T(8,128)(2,1)S(1)}, bf16[512,256]{1,0:T(8,128)(2,1)S(1)}, u32[]{:S(2)}, u32[]{:S(2)}) collective-permute-start(bf16[512,256]{1,0:T(8,128)(2,1)S(1)} %collective-permute-done.refs_1_), channel_id=1, source_target_pairs={{4,0},{8,4},{12,8},{16,12},{20,16},{24,20},{28,24},{0,28},{5,1},{9... | collective-permute-start | bytes 786440 | tf_op jit(solution)/shard_map/ppermute | solution.py:160
  119.9 15.4 %collective-permute-start.7 = (bf16[512,256]{1,0:T(8,128)(2,1)S(1)}, bf16[512,256]{1,0:T(8,128)(2,1)S(1)}, u32[]{:S(2)}, u32[]{:S(2)}) collective-permute-start(bf16[512,256]{1,0:T(8,128)(2,1)S(1)} %pad_maximum_fusion.1.refs_0_), channel_id=1, source_target_pairs={{4,0},{8,4},{12,8},{16,12},{20,16},{24,20},{28,24},{0,28},{5,1},{9... | collective-permute-start | bytes 786440 | tf_op jit(solution)/shard_map/ppermute | solution.py:160
  123.0 14.9 %collective-permute-start.11 = (bf16[512,256]{1,0:T(8,128)(2,1)S(1)}, bf16[512,256]{1,0:T(8,128)(2,1)S(1)}, u32[]{:S(2)}, u32[]{:S(2)}) collective-permute-start(bf16[512,256]{1,0:T(8,128)(2,1)S(1)} %pad_maximum_fusion.1.refs_0_), channel_id=1, source_target_pairs={{28,0},{0,4},{4,8},{8,12},{12,16},{16,20},{20,24},{24,28},{29,1},{... | collective-permute-start | bytes 786440 | tf_op jit(solution)/shard_map/ppermute | solution.py:160
  123.0 12.2 %collective-permute-start.5 = (bf16[512,256]{1,0:T(8,128)(2,1)S(1)}, bf16[512,256]{1,0:T(8,128)(2,1)S(1)}, u32[]{:S(2)}, u32[]{:S(2)}) collective-permute-start(bf16[512,256]{1,0:T(8,128)(2,1)S(1)} %collective-permute-done.4.refs_7_), channel_id=1, source_target_pairs={{28,0},{0,4},{4,8},{8,12},{12,16},{16,20},{20,24},{24,28},{29,1},{... | collective-permute-start | bytes 786440 | tf_op jit(solution)/shard_map/ppermute | solution.py:160
  123.0 14.9 %collective-permute-start.2 = (bf16[512,256]{1,0:T(8,128)(2,1)S(1)}, bf16[512,256]{1,0:T(8,128)(2,1)}, u32[]{:S(2)}, u32[]{:S(2)}) collective-permute-start(bf16[512,256]{1,0:T(8,128)(2,1)S(1)} %collective-permute-done.1.refs_2_), channel_id=1, source_target_pairs={{4,0},{8,4},{12,8},{16,12},{20,16},{24,20},{28,24},{0,28},{5,1},{9... | collective-permute-start | bytes 786440 | tf_op jit(solution)/shard_map/ppermute | solution.py:160
  135.3 11.4 %collective-permute-start.6 = (bf16[512,256]{1,0:T(8,128)(2,1)S(1)}, bf16[512,256]{1,0:T(8,128)(2,1)}, u32[]{:S(2)}, u32[]{:S(2)}) collective-permute-start(bf16[512,256]{1,0:T(8,128)(2,1)S(1)} %collective-permute-done.5.refs_6_), channel_id=1, source_target_pairs={{28,0},{0,4},{4,8},{8,12},{12,16},{16,20},{20,24},{24,28},{29,1},{... | collective-permute-start | bytes 786440 | tf_op jit(solution)/shard_map/ppermute | solution.py:160
  135.3 6.2 %collective-permute-start.8 = (bf16[512,256]{1,0:T(8,128)(2,1)S(1)}, bf16[512,256]{1,0:T(8,128)(2,1)S(1)}, u32[]{:S(2)}, u32[]{:S(2)}) collective-permute-start(bf16[512,256]{1,0:T(8,128)(2,1)S(1)} %collective-permute-done.7.refs_1_), channel_id=1, source_target_pairs={{4,0},{8,4},{12,8},{16,12},{20,16},{24,20},{28,24},{0,28},{5,1},{9... | collective-permute-start | bytes 786440 | tf_op jit(solution)/shard_map/ppermute | solution.py:160
  138.0 8.8 %collective-permute-start.12 = (bf16[512,256]{1,0:T(8,128)(2,1)S(1)}, bf16[512,256]{1,0:T(8,128)(2,1)S(1)}, u32[]{:S(2)}, u32[]{:S(2)}) collective-permute-start(bf16[512,256]{1,0:T(8,128)(2,1)S(1)} %collective-permute-done.11.refs_7_), channel_id=1, source_target_pairs={{28,0},{0,4},{4,8},{8,12},{12,16},{16,20},{20,24},{24,28},{29,1},{... | collective-permute-start | bytes 786440 | tf_op jit(solution)/shard_map/ppermute | solution.py:160
  138.0 8.8 %collective-permute-start.3 = (bf16[512,256]{1,0:T(8,128)(2,1)}, bf16[512,256]{1,0:T(8,128)(2,1)}, u32[]{:S(2)}, u32[]{:S(2)}) collective-permute-start(bf16[512,256]{1,0:T(8,128)(2,1)} %collective-permute-done.2.refs_3_), channel_id=1, source_target_pairs={{4,0},{8,4},{12,8},{16,12},{20,16},{24,20},{28,24},{0,28},{5,1},{9... | collective-permute-start | bytes 786440 | tf_op jit(solution)/shard_map/ppermute | solution.py:160
  141.5 45.4 %collective-permute-start.9 = (bf16[512,256]{1,0:T(8,128)(2,1)S(1)}, bf16[512,256]{1,0:T(8,128)(2,1)}, u32[]{:S(2)}, u32[]{:S(2)}) collective-permute-start(bf16[512,256]{1,0:T(8,128)(2,1)S(1)} %collective-permute-done.8.refs_2_), channel_id=1, source_target_pairs={{4,0},{8,4},{12,8},{16,12},{20,16},{24,20},{28,24},{0,28},{5,1},{9... | collective-permute-start | bytes 786440 | tf_op jit(solution)/shard_map/ppermute | solution.py:160
  146.7 54.4 %collective-permute-start.13 = (bf16[512,256]{1,0:T(8,128)(2,1)S(1)}, bf16[512,256]{1,0:T(8,128)(2,1)}, u32[]{:S(2)}, u32[]{:S(2)}) collective-permute-start(bf16[512,256]{1,0:T(8,128)(2,1)S(1)} %collective-permute-done.12.refs_6_), channel_id=1, source_target_pairs={{28,0},{0,4},{4,8},{8,12},{12,16},{16,20},{20,24},{24,28},{29,1},{... | collective-permute-start | bytes 786440 | tf_op jit(solution)/shard_map/ppermute | solution.py:160
  157.0 44.1 %all-to-all-start.1 = ((f32[8,1,8,128]{3,2,1,0:T(8,128)}), f32[8,1,8,128]{3,2,1,0:T(8,128)S(1)}, u32[]{:S(2)}, u32[]{:S(2)}) async-start(f32[8,1,8,128]{3,2,1,0:T(8,128)} %broadcast_in_dim.45), calls=%async_computation.1 | async-start | bytes 65536 | tf_op jit(solution)/shard_map/all_to_all | solution.py:175
  186.9 14.3 %collective-permute-start.10 = (bf16[512,256]{1,0:T(8,128)(2,1)}, bf16[512,256]{1,0:T(8,128)(2,1)}, u32[]{:S(2)}, u32[]{:S(2)}) collective-permute-start(bf16[512,256]{1,0:T(8,128)(2,1)} %collective-permute-done.9.refs_3_), channel_id=1, source_target_pairs={{4,0},{8,4},{12,8},{16,12},{20,16},{24,20},{28,24},{0,28},{5,1},{9... | collective-permute-start | bytes 786440 | tf_op jit(solution)/shard_map/ppermute | solution.py:160
  201.1 9.8 %copy-start.7 = (bf16[1,512,1024]{2,1,0:T(8,128)(2,1)S(1)}, bf16[1,512,1024]{2,1,0:T(8,128)(2,1)}, u32[]{:S(2)}) copy-start(bf16[1,512,1024]{2,1,0:T(8,128)(2,1)} %all-gather.12.cloned.1.call-done) | copy-start | bytes 3145732
  211.0 2.3 copy-start.6
  214.4 50.0 %copy-start.5 = (bf16[1,128,1024]{2,1,0:T(8,128)(2,1)S(1)}, bf16[1,128,1024]{2,1,0:T(8,128)(2,1)}, u32[]{:S(2)}) copy-start(bf16[1,128,1024]{2,1,0:T(8,128)(2,1)} %param.8) | copy-start | bytes 786436
  215.7 48.7 %copy-start.3 = (bf16[512,1024]{1,0:T(8,128)(2,1)S(1)}, bf16[512,1024]{1,0:T(8,128)(2,1)}, u32[]{:S(2)}) copy-start(bf16[512,1024]{1,0:T(8,128)(2,1)} %all-gather.8.cloned.1.call-done) | copy-start | bytes 3145732
  215.7 55.3 %copy-start.4 = (bf16[1,128,1024]{2,1,0:T(8,128)(2,1)S(1)}, bf16[1,128,1024]{2,1,0:T(8,128)(2,1)}, u32[]{:S(2)}) copy-start(bf16[1,128,1024]{2,1,0:T(8,128)(2,1)} %param.9) | copy-start | bytes 786436
  215.7 34.9 %all-to-all-start.3 = ((bf16[64,64,128]{2,1,0:T(8,128)(2,1)}), bf16[64,64,128]{2,1,0:T(8,128)(2,1)S(1)}, u32[]{:S(2)}, u32[]{:S(2)}) async-start(bf16[64,64,128]{2,1,0:T(8,128)(2,1)} %bitcast.45), calls=%async_computation.3 | async-start | bytes 2097152 | tf_op jit(solution)/shard_map/all_to_all | solution.py:275
  251.5 8.8 %all-to-all-start.4 = ((f32[4,4,384]{2,1,0:T(4,128)}), f32[4,4,384]{2,1,0:T(4,128)S(1)}, u32[]{:S(2)}, u32[]{:S(2)}) async-start(f32[4,4,384]{2,1,0:T(4,128)} %reshape.77), calls=%async_computation.4 | async-start | bytes 49152 | tf_op jit(solution)/shard_map/all_to_all | solution.py:279
  260.2 10.8 %all-to-all-start.2 = ((bf16[4,128,384]{2,1,0:T(8,128)(2,1)}), bf16[4,128,384]{2,1,0:T(8,128)(2,1)S(1)}, u32[]{:S(2)}, u32[]{:S(2)}) async-start(bf16[4,128,384]{2,1,0:T(8,128)(2,1)} %bitcast.16), calls=%async_computation.2 | async-start | bytes 786432 | tf_op jit(solution)/shard_map/all_to_all | solution.py:262
  271.0 3.2 %copy-start.2 = (bf16[4,1024,384]{2,1,0:T(8,128)(2,1)S(1)}, bf16[4,1024,384]{2,1,0:T(8,128)(2,1)}, u32[]{:S(2)}) copy-start(bf16[4,1024,384]{2,1,0:T(8,128)(2,1)} %all-gather.10.cloned.1.call-done) | copy-start | bytes 9437188
Sparse Core Ops, SparseCore 0:
  9.8 27.4 all-gather.11
  39.1 25.7 all-gather.13
  67.5 50.5 all-gather.7
  141.2 42.8 all-gather.9

commit v2 on v1

v2 whole, which is shorter than its diff:
```python
import functools
import math

import jax
import jax.numpy as jnp
from jax import lax
from jax.experimental import pallas as pl
from jax.experimental.pallas import tpu as pltpu
from jax.sharding import Mesh
from jax.sharding import PartitionSpec as P

HEADS = 4
HD = 128
SPAN = 64
NF = 8
NZ = 8
ROWS = 512
NEG = -1e30
SCALE = 1.0 / math.sqrt(HD)
C2 = SCALE * math.log2(math.e)
FLOPS = 8
VMEM_LIMIT = 40 << 20
BF = jnp.bfloat16
F32 = jnp.float32


def dot(a, b):
    return jnp.dot(a, b, preferred_element_type=F32)


def dot_nt(a, b):
    return lax.dot_general(a, b, (((1,), (1,)), ((), ())), preferred_element_type=F32)


def dot_tn(a, b):
    return lax.dot_general(a, b, (((0,), (0,)), ((), ())), preferred_element_type=F32)


def with_bias(s, bias_ref, firsts):
    parts = []
    for t in range(ROWS // SPAN):
        row = jnp.concatenate([bias_ref[first + t] for first in firsts], axis=1)
        parts.append(s[t * SPAN : (t + 1) * SPAN, :] + row)
    return jnp.concatenate(parts, axis=0)


def tiles(s):
    return [s[:, t * HD : (t + 1) * HD] for t in range(s.shape[1] // HD)]


def wide(row, count):
    return jnp.concatenate([row] * (count * (ROWS // HD)), axis=1)


class Staged:
    def __init__(self, chunks, buf, sems, at_once):
        self.buf, self.sems, self.at_once = buf, sems, at_once
        self.turns = len(chunks) // at_once
        self.copies = [
            pltpu.make_async_copy(
                chunk, buf.at[n // at_once, pl.ds(n % at_once * ROWS, ROWS)], sems.at[n]
            )
            for n, chunk in enumerate(chunks)
        ]
        for copy in self.copies:
            copy.start()

    def turn(self, n):
        for i in range(self.at_once):
            pltpu.make_async_copy(
                self.buf.at[n, pl.ds(i * ROWS, ROWS)],
                self.buf.at[n, pl.ds(i * ROWS, ROWS)],
                self.sems.at[n * self.at_once + i],
            ).wait()
        return self.buf.at[n]


def forward_kernel(count, at_once, first, last, number_ref, *refs):
    q_ref, refs = refs[0], refs[1:]
    chunks, refs = refs[:count], refs[count:]
    bias_ref, refs = refs[0], refs[1:]
    if not first:
        state_in, refs = refs[0], refs[1:]
    if last:
        g_ref, o_ref, stat_ref, row_ref, state, buf, sems = refs
    else:
        state, buf, sems = refs
    blocks = Staged(chunks, buf, sems, at_once)
    if first:
        state[0] = jnp.full_like(state[0], NEG)
        state[1] = jnp.zeros_like(state[1])
        state[2] = jnp.zeros_like(state[2])
    else:
        state[...] = state_in[...]

    @pl.loop(0, blocks.turns)
    def _(n):
        kv = blocks.turn(n)
        s = dot_nt(q_ref[...], kv[:, :HD]) * C2
        s = with_bias(s, bias_ref, [number_ref[n * at_once + i] * 8 for i in range(at_once)])
        old = state[0]
        top = functools.reduce(jnp.maximum, tiles(s))
        new = jnp.maximum(old, jnp.max(top, axis=1, keepdims=True))
        fade = jnp.exp2(old - new)
        e = jnp.exp2(s - wide(new, at_once))
        state[0] = new
        state[1] = state[1] * fade + sum(tiles(e))
        state[2] = state[2] * fade + dot(e.astype(BF), kv[:, HD:])

    if last:
        total = jnp.sum(state[1], axis=1, keepdims=True)
        combined = state[2] * (1.0 / total)
        o_ref[...] = combined.astype(BF)
        lse = state[0] + jnp.log2(total)
        delta = jnp.sum(combined * g_ref[...].astype(F32), axis=1, keepdims=True)
        delta = jnp.broadcast_to(delta, (ROWS, HD))
        row_ref[0] = lse
        row_ref[1] = delta
        stat_ref[0:1, :] = lse.T[0:1, :]
        stat_ref[1:2, :] = delta.T[0:1, :]


def query_kernel(count, at_once, q_ref, g_ref, row_ref, *refs):
    chunks, (bias_ref, dq_ref, acc, buf, sems) = refs[:count], refs[count:]
    blocks = Staged(chunks, buf, sems, at_once)
    acc[...] = jnp.zeros_like(acc)

    @pl.loop(0, blocks.turns)
    def _(n):
        kv = blocks.turn(n)
        s = dot_nt(q_ref[...], kv[:, :HD]) * C2
        s = with_bias(s, bias_ref, [(n * at_once + i) * 8 for i in range(at_once)])
        p = jnp.exp2(s - wide(row_ref[0], at_once))
        dp = dot_nt(g_ref[...], kv[:, HD:])
        ds = (p * (dp - wide(row_ref[1], at_once))).astype(BF)
        acc[...] += dot(ds, kv[:, :HD])

    dq_ref[...] = (acc[...] * SCALE).astype(BF)


def key_kernel(count, at_once, first, last, number_ref, kv_ref, stat_ref, *refs):
    chunks, refs = refs[:count], refs[count:]
    bias_ref, refs = refs[0], refs[1:]
    if not first:
        state_in, refs = refs[0], refs[1:]
    if last:
        d_ref, state, buf, sems = refs
    else:
        state, buf, sems = refs
    blocks = Staged(chunks, buf, sems, at_once)
    if first:
        state[...] = jnp.zeros_like(state)
    else:
        state[...] = state_in[...]

    @pl.loop(0, blocks.turns)
    def _(n):
        qg = blocks.turn(n)
        numbers = [number_ref[n * at_once + i] for i in range(at_once)]
        lse = jnp.concatenate([stat_ref[d, 0:1, :] for d in numbers], axis=1)
        delta = jnp.concatenate([stat_ref[d, 1:2, :] for d in numbers], axis=1)
        s = dot_nt(kv_ref[:, :HD], qg[:, :HD]) * C2
        s = with_bias(s, bias_ref, [d * 8 for d in numbers])
        p = jnp.exp2(s - lse)
        dp = dot_nt(kv_ref[:, HD:], qg[:, HD:])
        ds = (p * (dp - delta)).astype(BF)
        state[0] += dot(ds, qg[:, :HD])
        state[1] += dot(p.astype(BF), qg[:, HD:])

    if last:
        d_ref[:, :HD] = (state[0] * SCALE).astype(BF)
        d_ref[:, HD:] = state[1].astype(BF)


def call(kernel, name, out_shape, scratch, flops, *args):
    many = isinstance(out_shape, tuple)
    vmem = pl.BlockSpec(memory_space=pltpu.VMEM)
    smem = pl.BlockSpec(memory_space=pltpu.SMEM)
    return pl.pallas_call(
        kernel,
        name=name,
        out_shape=out_shape,
        in_specs=[smem if a.dtype == jnp.int32 else vmem for a in args],
        out_specs=(vmem,) * len(out_shape) if many else vmem,
        scratch_shapes=scratch,
        compiler_params=pltpu.CompilerParams(vmem_limit_bytes=VMEM_LIMIT),
        cost_estimate=pl.CostEstimate(
            flops=flops, bytes_accessed=1 << 20, transcendentals=flops // 2560
        ),
    )(*args)


def take(x, axis, size, by):
    return lax.ppermute(x, axis, [((i + by) % size, i) for i in range(size)])


def swap(x, bit):
    return lax.ppermute(x, "h", [(i, i ^ bit) for i in range(HEADS)])


def gather(x):
    far = swap(x, 2)
    return jnp.concatenate([x, swap(x, 1), far, swap(far, 1)], axis=0)


def add_heads(terms):
    blocks = terms.reshape(HEADS, ROWS // HEADS, terms.shape[1])
    near = swap(jnp.stack([blocks[1], blocks[3]]).astype(BF), 1).astype(F32)
    return blocks[0] + near[0] + swap((blocks[2] + near[1]).astype(BF), 2).astype(F32)


def after(x, *others):
    return lax.optimization_barrier((x,) + others)[0]


def exchange(x, axis):
    return lax.all_to_all(x, axis, split_axis=0, concat_axis=0, tiled=True)


def ring(x):
    out = [None] * NZ
    out[0] = x
    for r in range(1, NZ // 2 + 1):
        out[r] = take(out[r - 1], "z", NZ, 1)
        if r < NZ // 2:
            out[-r] = take(out[(-r + 1) % NZ], "z", NZ, -1)
    return out


def spread(x, axis, size):
    return exchange(jnp.broadcast_to(x[None], (size,) + x.shape), axis)


def span_bias(block_mask, span_order, z, h):
    order = jnp.tile(span_order.reshape(NZ, 2, 2, 2), (2, 1, 1, 1))
    order = lax.dynamic_slice(order, (z, 0, 0, 0), (NZ, 2, 2, 2))
    order = jnp.where(h // 2 == 1, order[:, ::-1], order)
    order = jnp.where(h % 2 == 1, order[:, :, ::-1], order).reshape(64) // 2
    hot = (order[:, None] == jnp.arange(32, dtype=jnp.int32)[None, :]).astype(F32)
    linked = dot(dot(hot, block_mask.astype(F32)), hot.T)
    bias = jnp.where(linked > 0.5, 0.0, NEG).astype(F32)
    of_queries = jnp.transpose(bias[:8].reshape(8, NZ, 8), (1, 0, 2)).reshape(64, 8)
    of_keys = jnp.transpose(bias[:, :8].reshape(NZ, 8, 8), (0, 2, 1)).reshape(64, 8)
    both = jnp.repeat(jnp.concatenate([of_queries, of_keys]), SPAN, axis=1)
    return both[:64, None, :], both[64:, None, :]


def body(tokens, cotangent, w_query, w_key, w_value, w_out, block_mask, span_order):
    x_own = tokens[0]
    dy_own = cotangent[0]
    h = lax.axis_index("h")
    z = lax.axis_index("z")
    bias_q, bias_k = span_bias(block_mask, span_order, z, h)

    def head(w):
        return lax.dynamic_slice(w, (0, h * HD), (w.shape[0], HD))

    pairs = [(f * HEADS + i, (4 * (f % 2) + i) * HEADS + f // 2) for f in range(NF) for i in range(HEADS)]
    w_part = lax.ppermute(lax.dynamic_slice(w_out, (h * 16, 0), (16, 1024)), ("f", "h"), pairs)
    x = gather(x_own)
    mine = [head(w_key), head(w_value), head(w_query), w_part.reshape(HD, HD)]
    w_got = spread(jnp.concatenate(mine, axis=1), "f", NF).reshape(1024, 4 * HD)
    w_head = w_got[:, : 3 * HD]

    kv = dot(x, w_head[:, : 2 * HD]).astype(BF)
    q = dot(x, w_head[:, 2 * HD :]).astype(BF)
    kv_all = ring(kv)

    dy = gather(after(dy_own, x))
    out_head = w_got[:, 3 * HD :].reshape(HD, 1024)
    g = dot_nt(dy, out_head).astype(BF)
    qg_all = ring(jnp.concatenate([q, g], axis=1))

    work = FLOPS * ROWS * ROWS * HD
    head_rows = jax.ShapeDtypeStruct((ROWS, HD), BF)
    state_shape = (3, ROWS, HD)

    def staging(count, at_once):
        blocks = pltpu.VMEM((count // at_once, at_once * ROWS, 2 * HD), BF)
        return [blocks, pltpu.SemaphoreType.DMA((count,))]

    state = ()
    for number in ((0,), (1, 7), (2, 6), (3, 5)):
        count = len(number)
        state = (
            call(
                functools.partial(forward_kernel, count, count, not state, False),
                "attn_forward",
                jax.ShapeDtypeStruct(state_shape, F32),
                staging(count, count),
                2 * work * count,
                jnp.array(number, jnp.int32),
                q,
                *[kv_all[d] for d in number],
                bias_q,
                *state,
            ),
        )
    att, stat, row = call(
        functools.partial(forward_kernel, 1, 1, False, True),
        "attn_forward_end",
        (
            head_rows,
            jax.ShapeDtypeStruct((2, ROWS), F32),
            jax.ShapeDtypeStruct((2, ROWS, HD), F32),
        ),
        [pltpu.VMEM(state_shape, F32)] + staging(1, 1),
        2 * work,
        jnp.array((4,), jnp.int32),
        q,
        kv_all[4],
        bias_q,
        *state,
        g,
    )
    stats = spread(stat.reshape(1, 8, 128), "z", NZ)
    dq = call(
        functools.partial(query_kernel, NZ, 2),
        "attn_query_side",
        head_rows,
        [pltpu.VMEM((ROWS, HD), F32)] + staging(NZ, 2),
        3 * work * NZ,
        q,
        g,
        row,
        *kv_all,
        bias_q,
    )

    mixed = (x_own.astype(F32) + add_heads(dot(att, out_head))).astype(BF)

    def scatter(terms):
        return jnp.sum(exchange(terms, ("f", "z")).astype(F32), axis=0)

    moved = jnp.arange(HD, dtype=jnp.int32).reshape(2, 4, NZ, 2)
    moved = (moved // 64) * 64 + (moved // 2 % 8) * 8 + (moved // 16 % 4) * 2 + moved % 2
    move = (jnp.arange(HD, dtype=jnp.int32)[:, None] == moved.reshape(1, HD)).astype(BF)
    grad_o = dot_tn(dot(att, move).astype(BF), dy).astype(BF)
    early_terms = jnp.concatenate(
        [grad_o.reshape(64, 16, 128), dot_tn(x, dq).astype(BF).reshape(64, 16, HD)], axis=1
    )
    early = scatter(early_terms)

    stats = after(stats, early_terms).reshape(NZ, 2, ROWS)
    stats = lax.dynamic_slice(jnp.concatenate([stats, stats]), (z, 0, 0), (NZ, 2, ROWS))
    acc_shape = (2, ROWS, HD)
    number = (0, 1, 7, 2, 6, 3)
    part = call(
        functools.partial(key_kernel, len(number), 2, True, False),
        "attn_key_side",
        jax.ShapeDtypeStruct(acc_shape, F32),
        staging(len(number), 2),
        4 * work * len(number),
        jnp.array(number, jnp.int32),
        kv,
        stats,
        *[qg_all[d] for d in number],
        bias_k,
    )
    stats = after(stats, early, mixed)
    number = (5, 4)
    dkv = call(
        functools.partial(key_kernel, len(number), 2, False, True),
        "attn_key_side_end",
        jax.ShapeDtypeStruct((ROWS, 2 * HD), BF),
        [pltpu.VMEM(acc_shape, F32)] + staging(len(number), 2),
        4 * work * len(number),
        jnp.array(number, jnp.int32),
        kv,
        stats,
        *[qg_all[d] for d in number],
        bias_k,
        part,
    )
    pairs = [((4 * e + i) * 4 + a, (2 * a + e) * 4 + i) for e in range(2) for i in range(4) for a in range(4)]
    grad_o = lax.ppermute(early[:16], ("f", "h"), pairs).reshape(2, 1024)
    grad_q = early[16:]

    late_terms = dot_tn(x, dkv).astype(BF).reshape(64, 16, 2 * HD)
    late = scatter(late_terms)
    d_head = jnp.concatenate([after(dkv, late_terms), dq], axis=1)
    token_grad = (dy_own.astype(F32) + add_heads(dot_nt(d_head, w_head))).astype(BF)

    grads = jnp.concatenate([grad_q, late], axis=1).reshape(HEADS, 4, 3 * HD)
    grads = exchange(grads, "h").reshape(HEADS, 4, 3, HD)
    grads = jnp.transpose(grads, (2, 1, 0, 3)).reshape(3, 4, HEADS * HD)
    return (mixed[None], token_grad[None], grads[0], grads[1], grads[2], grad_o)


def solution(mesh):
    fine = Mesh(mesh.devices.reshape(NF, NZ, HEADS), ("f", "z", "h"))
    rows = P("f", ("z", "h"), None)
    split = P(("f", "z", "h"), None)
    return jax.shard_map(
        body,
        mesh=fine,
        in_specs=(rows, rows, P("f", None), P("f", None), P("f", None), P("f", None), P(), P()),
        out_specs=(rows, rows, split, split, split, split),
        check_vma=False,
    )
```

time: 283 us -> 198 us (0.70)
  waiting for transfers between devices: 123 us -> 40.5 us
  starting transfers between devices: 46.7 us -> 88.1 us
  blocking collectives: 37.9 us -> 0 us
  between operations: 14.1 us -> 1.28 us
  other arithmetic: 2.43 us -> 13.3 us
  Pallas kernels: 28 us -> 20 us
  local copies, waits for them, and re-layouts: 15.4 us -> 20.8 us
    all_gather x4 -> x0, waiting for transfers between devices: 71.6 us -> none  [the longest x1 53.2 us: body(): out_full = lax.all_gather(w_out, 'f', axis=0, tiled=True)]
    all_to_all x4 -> x5, waiting for transfers between devices: 33.8 us -> 7.9 us  [exchange(): return lax.all_to_all(x, axis, split_axis=0, concat_axis=0, tiled=True)]
    all_to_all x4 -> x5, starting transfers between devices: 20.9 us -> 43.1 us  [exchange(): return lax.all_to_all(x, axis, split_axis=0, concat_axis=0, tiled=True)]
    all_to_all x1 -> x0, blocking collectives: 20.1 us -> none  [spread(): return lax.all_to_all(many, axis, split_axis=0, concat_axis=0, tiled=True)]
    ppermute x14 -> x26, starting transfers between devices: 25.6 us -> 45 us  [the longest x14 27.6 us: take(): return lax.ppermute(x, axis, [((i + by) % size, i) for i in range(size)])]
    all_gather x1 -> x0, blocking collectives: 17.8 us -> none  [body(): att_all = lax.all_gather(att[None], 'h', axis=0, tiled=True)]
    ppermute x14 -> x26, waiting for transfers between devices: 15.4 us -> 32.6 us  [the longest x10 23.4 us: swap(): return lax.ppermute(x, 'h', [(i, i ^ bit) for i in range(HEADS)])]
    pallas_call x3 -> x8, Pallas kernels: 28 us -> 20 us  [call(): pl.pallas_call(kernel, name=name, out_shape=out_shape, in_specs=[smem if...]
  transfers between devices with their start and end apart: 22 -> 31, of which waited for: 9 -> 12; matrix products, arithmetic and copies ran while one was open for 10% -> 21% of each run, Pallas kernels for 10% -> 9%
where the time goes in v2:
time: 198 us; the launch traced here: 196 us
  starting transfers between devices  88.1 us (44%)
  waiting for transfers between devices  40.5 us (20%)
  local copies, waits for them, and re-layouts  20.8 us (11%)
  Pallas kernels  20 us (10%)
  other arithmetic  13.3 us (7%)
  matrix products  12.1 us (6%)
    all_to_all x5, starting transfers between devices, exchange(): return lax.all_to_all(x, axis, split_axis=0, concat_axis=0, tiled=True)  43.1 us
    ppermute x14, starting transfers between devices, take(): return lax.ppermute(x, axis, [((i + by) % size, i) for i in range(size)])  27.6 us
    ppermute x10, waiting for transfers between devices, swap(): return lax.ppermute(x, 'h', [(i, i ^ bit) for i in range(HEADS)])  23.4 us
    pallas_call x8, Pallas kernels, call(): pl.pallas_call(kernel, name=name, out_shape=out_shape, in_specs=[smem if...  20 us
    ppermute x10, starting transfers between devices, swap(): return lax.ppermute(x, 'h', [(i, i ^ bit) for i in range(HEADS)])  9.4 us
    all_to_all x5, waiting for transfers between devices, exchange(): return lax.all_to_all(x, axis, split_axis=0, concat_axis=0, tiled=True)  7.9 us
    ppermute x14, waiting for transfers between devices, take(): return lax.ppermute(x, axis, [((i + by) % size, i) for i in range(size)])  7.35 us
    unnamed x47, local copies, waits for them, and re-layouts  5.68 us
  transfers between devices with their start and end apart: 31, of which 12 were waited for; matrix products, arithmetic and copies ran while one was open for 21% of the time, Pallas kernels for 9%

profile of v2, /device:TPU:1, one launch (start us, length us, event | category | flops | bytes accessed | tf_op | source)
XLA Modules:
  0.0 196.1 jit_solution(13710094303263444670)
XLA Ops:
  0.7 2.1 %collective-permute-start.1 = (bf16[128,1024]{1,0:T(8,128)(2,1)}, bf16[128,1024]{1,0:T(8,128)(2,1)S(1)}, u32[]{:S(2)}, u32[]{:S(2)}) collective-permute-start(bf16[128,1024]{1,0:T(8,128)(2,1)} %bitcast.97), channel_id=1, source_target_pairs={{0,2},{1,3},{2,0},{3,1},{4,6},{5,7},{6,4},{7,5},{8,10},{9,11},{10,... | collective-permute-start | bytes 786440 | tf_op jit(solution)/shard_map/ppermute | solution.py:198
  2.8 1.3 collective-permute-start
  4.1 2.7 %collective-permute-start.3 = (bf16[16,1024]{1,0:T(8,128)(2,1)S(1)}, bf16[16,1024]{1,0:T(8,128)(2,1)S(1)}, u32[]{:S(2)}, u32[]{:S(2)}) collective-permute-start(bf16[16,1024]{1,0:T(8,128)(2,1)S(1)} %constant_dynamic-slice_fusion.1), channel_id=1, source_target_pairs={{0,0},{1,32},{2,64},{3,96},{32,128},{33,160},{34,192},{35,224},{64... | collective-permute-start | bytes 98312 | tf_op jit(solution)/shard_map/ppermute | solution.py:259
  8.0 0.8 constant_dynamic-slice_fusion.2
  9.7 1.1 collective-permute-done.3
  11.0 1.1 broadcast_in_dim.41
  12.1 7.8 %all-to-all-start = ((bf16[8,128,512]{2,1,0:T(8,128)(2,1)}), bf16[8,128,512]{2,1,0:T(8,128)(2,1)S(1)}, u32[]{:S(2)}, u32[]{:S(2)}) async-start(bf16[8,128,512]{2,1,0:T(8,128)(2,1)} %broadcast_in_dim.41), calls=%async_computation | async-start | bytes 2097152 | tf_op jit(solution)/shard_map/all_to_all | solution.py:217
  19.9 1.0 pad_maximum_fusion
  22.4 15.1 %collective-permute-done.12 = bf16[128,1024]{1,0:T(8,128)(2,1)} collective-permute-done((bf16[128,1024]{1,0:T(8,128)(2,1)S(1)}, bf16[128,1024]{1,0:T(8,128)(2,1)}, u32[]{:S(2)}, u32[]{:S(2)}) %collective-permute-start.12) | collective-permute-done | bytes 262176 | tf_op jit(solution)/shard_map/ppermute | solution.py:198
  37.5 0.8 collective-permute-start.13
  39.1 1.7 constant_dynamic-update-slice_fusion.1
  40.7 1.0 copy-done.13
  42.2 5.7 %collective-permute-start.4 = (bf16[512,256]{1,0:T(8,128)(2,1)S(1)}, bf16[512,256]{1,0:T(8,128)(2,1)S(1)}, u32[]{:S(2)}, u32[]{:S(2)}) collective-permute-start(bf16[512,256]{1,0:T(8,128)(2,1)S(1)} %convolution_convert_fusion.3.refs_1_.refs_0_.kv_ref), channel_id=1, source_target_pairs={{4,0},{8,4},{12,8},{16,12},{20,16},{24,20},{28,24},{0,28},{5,1},{9... | collective-permute-start | bytes 786440 | tf_op jit(solution)/shard_map/ppermute | solution.py:194
  47.8 1.0 slice.130
  48.9 1.5 convolution_convert_fusion.6.refs_0_.q_ref
  50.4 1.7 constant_dynamic-update-slice_fusion
  52.1 1.7 convolution_convert_fusion.5.refs_4_.g_ref
  53.8 2.8 %collective-permute-start.19 = (bf16[512,256]{1,0:T(8,128)(2,1)S(1)}, bf16[512,256]{1,0:T(8,128)(2,1)S(1)}, u32[]{:S(2)}, u32[]{:S(2)}) collective-permute-start(bf16[512,256]{1,0:T(8,128)(2,1)S(1)} %pad_maximum_fusion.4.refs_0_), channel_id=1, source_target_pairs={{4,0},{8,4},{12,8},{16,12},{20,16},{24,20},{28,24},{0,28},{5,1},{9... | collective-permute-start | bytes 786440 | tf_op jit(solution)/shard_map/ppermute | solution.py:194
  56.6 2.7 %collective-permute-start.5 = (bf16[512,256]{1,0:T(8,128)(2,1)S(1)}, bf16[512,256]{1,0:T(8,128)(2,1)S(1)}, u32[]{:S(2)}, u32[]{:S(2)}) collective-permute-start(bf16[512,256]{1,0:T(8,128)(2,1)S(1)} %collective-permute-done.4.refs_1_), channel_id=1, source_target_pairs={{4,0},{8,4},{12,8},{16,12},{20,16},{24,20},{28,24},{0,28},{5,1},{9... | collective-permute-start | bytes 786440 | tf_op jit(solution)/shard_map/ppermute | solution.py:194
  59.4 2.3 %collective-permute-done.19.refs_1_ = bf16[512,256]{1,0:T(8,128)(2,1)S(1)} collective-permute-done((bf16[512,256]{1,0:T(8,128)(2,1)S(1)}, bf16[512,256]{1,0:T(8,128)(2,1)S(1)}, u32[]{:S(2)}, u32[]{:S(2)}) %collective-permute-start.19) | collective-permute-done | bytes 262176 | tf_op jit(solution)/shard_map/ppermute | solution.py:194
  61.7 3.4 %collective-permute-start.20 = (bf16[512,256]{1,0:T(8,128)(2,1)S(1)}, bf16[512,256]{1,0:T(8,128)(2,1)S(1)}, u32[]{:S(2)}, u32[]{:S(2)}) collective-permute-start(bf16[512,256]{1,0:T(8,128)(2,1)S(1)} %collective-permute-done.19.refs_1_), channel_id=1, source_target_pairs={{4,0},{8,4},{12,8},{16,12},{20,16},{24,20},{28,24},{0,28},{5,1},{9... | collective-permute-start | bytes 786440 | tf_op jit(solution)/shard_map/ppermute | solution.py:194
  65.1 2.2 %collective-permute-done.5.refs_1_.refs_2_ = bf16[512,256]{1,0:T(8,128)(2,1)S(1)} collective-permute-done((bf16[512,256]{1,0:T(8,128)(2,1)S(1)}, bf16[512,256]{1,0:T(8,128)(2,1)S(1)}, u32[]{:S(2)}, u32[]{:S(2)}) %collective-permute-start.5) | collective-permute-done | bytes 262176 | tf_op jit(solution)/shard_map/ppermute | solution.py:194
  67.3 3.4 %collective-permute-start.6 = (bf16[512,256]{1,0:T(8,128)(2,1)S(1)}, bf16[512,256]{1,0:T(8,128)(2,1)}, u32[]{:S(2)}, u32[]{:S(2)}) collective-permute-start(bf16[512,256]{1,0:T(8,128)(2,1)S(1)} %collective-permute-done.5.refs_1_.refs_2_), channel_id=1, source_target_pairs={{4,0},{8,4},{12,8},{16,12},{20,16},{24,20},{28,24},{0,28},{5,1},{9... | collective-permute-start | bytes 786440 | tf_op jit(solution)/shard_map/ppermute | solution.py:194
  72.9 3.4 %collective-permute-start.21 = (bf16[512,256]{1,0:T(8,128)(2,1)S(1)}, bf16[512,256]{1,0:T(8,128)(2,1)S(1)}, u32[]{:S(2)}, u32[]{:S(2)}) collective-permute-start(bf16[512,256]{1,0:T(8,128)(2,1)S(1)} %collective-permute-done.20.refs_3_), channel_id=1, source_target_pairs={{4,0},{8,4},{12,8},{16,12},{20,16},{24,20},{28,24},{0,28},{5,1},{9... | collective-permute-start | bytes 786440 | tf_op jit(solution)/shard_map/ppermute | solution.py:194
  76.3 2.2 %collective-permute-done.6.refs_1_.refs_3_ = bf16[512,256]{1,0:T(8,128)(2,1)} collective-permute-done((bf16[512,256]{1,0:T(8,128)(2,1)S(1)}, bf16[512,256]{1,0:T(8,128)(2,1)}, u32[]{:S(2)}, u32[]{:S(2)}) %collective-permute-start.6) | collective-permute-done | bytes 262176 | tf_op jit(solution)/shard_map/ppermute | solution.py:194
  78.5 3.5 %collective-permute-start.7 = (bf16[512,256]{1,0:T(8,128)(2,1)}, bf16[512,256]{1,0:T(8,128)(2,1)S(1)}, u32[]{:S(2)}, u32[]{:S(2)}) collective-permute-start(bf16[512,256]{1,0:T(8,128)(2,1)} %collective-permute-done.6.refs_1_.refs_3_), channel_id=1, source_target_pairs={{4,0},{8,4},{12,8},{16,12},{20,16},{24,20},{28,24},{0,28},{5,1},{9... | collective-permute-start | bytes 786440 | tf_op jit(solution)/shard_map/ppermute | solution.py:194
  82.0 1.6 attn_forward.5.refs_4_
  83.7 2.0 %attn_forward.6.refs_4_ = f32[3,512,128]{2,1,0:T(8,128)S(1)} custom-call(s32[2]{0:T(128)S(1)} %copy-done.6, bf16[512,128]{1,0:T(8,128)(2,1)S(1)} %convolution_convert_fusion.6.refs_0_.q_ref, bf16[512,256]{1,0:T(8,128)(2,1)S(1)} %collective-permute-done.5.refs_1_.refs_2_, bf16[512,256]{1,0:T(8,128)(2,1)} %collective-permute-done.9.refs_2_.refs_6_, ...), custom_call_target="tpu_custom_call" | custom-call | flops 1073741824 | bytes 1048576 | tf_op jit(solution)/shard_map/attn_forward/pallas_call | solution.py:179
  85.8 2.1 %attn_forward.7.refs_3_ = f32[3,512,128]{2,1,0:T(8,128)S(1)} custom-call(s32[2]{0:T(128)S(1)} %copy-done.5, bf16[512,128]{1,0:T(8,128)(2,1)S(1)} %convolution_convert_fusion.6.refs_0_.q_ref, bf16[512,256]{1,0:T(8,128)(2,1)} %collective-permute-done.6.refs_1_.refs_3_, bf16[512,256]{1,0:T(8,128)(2,1)} %collective-permute-done.10.refs_2_.refs_5_, ...), custom_call_target="tpu_custom_call" | custom-call | flops 1073741824 | bytes 1048576 | tf_op jit(solution)/shard_map/attn_forward/pallas_call | solution.py:179
  87.9 2.7 %collective-permute-start.22 = (bf16[512,256]{1,0:T(8,128)(2,1)S(1)}, bf16[512,256]{1,0:T(8,128)(2,1)}, u32[]{:S(2)}, u32[]{:S(2)}) collective-permute-start(bf16[512,256]{1,0:T(8,128)(2,1)S(1)} %collective-permute-done.21.refs_5_), channel_id=1, source_target_pairs={{4,0},{8,4},{12,8},{16,12},{20,16},{24,20},{28,24},{0,28},{5,1},{9... | collective-permute-start | bytes 786440 | tf_op jit(solution)/shard_map/ppermute | solution.py:194
  90.6 1.0 attn_forward_end.1
  92.3 0.8 copy-done.8
  93.1 2.1 %fusion.39 = (bf16[512,1024]{1,0:T(8,128)(2,1)}, f32[512,1024]{1,0:T(8,128)}) fusion(bf16[512,128]{1,0:T(8,128)(2,1)S(1)} %get-tuple-element.14, bf16[128,1024]{1,0:T(8,128)(2,1)S(1)} %copy-done.15), kind=kOutput, calls=%fused_computation.102 | convolution fusion | flops 134742016 | bytes 3538944 | tf_op jit(solution)/shard_map/dot_general | solution.py:28
  95.2 2.4 %convolution_convert_fusion.2 = bf16[128,1024]{1,0:T(8,128)(2,1)} fusion(bf16[512,1024]{1,0:T(8,128)(2,1)} %constant_dynamic-update-slice_fusion, bf16[512,128]{1,0:T(8,128)(2,1)S(1)} %get-tuple-element.14, s32[128]{0:T(128)S(1)} %fusion.30), kind=kOutput, calls=%fused_computation.2 | convolution fusion | flops 151207936 | bytes 1442304 | tf_op jit(solution)/shard_map/dot_general | solution.py:36
  97.6 1.8 reshape.280
  100.0 3.8 %all-to-all-start.1 = ((f32[8,1,8,128]{3,2,1,0:T(8,128)}), f32[8,1,8,128]{3,2,1,0:T(8,128)S(1)}, u32[]{:S(2)}, u32[]{:S(2)}) async-start(f32[8,1,8,128]{3,2,1,0:T(8,128)} %broadcast_in_dim.48), calls=%async_computation.1 | async-start | bytes 65536 | tf_op jit(solution)/shard_map/all_to_all | solution.py:217
  103.8 1.1 slice_bitcast_fusion.7
  105.0 0.8 pad_maximum_fusion.1
  105.8 2.8 %collective-permute-start.14 = (bf16[2,128,1024]{2,1,0:T(8,128)(2,1)}, bf16[2,128,1024]{2,1,0:T(8,128)(2,1)}, u32[]{:S(2)}, u32[]{:S(2)}) collective-permute-start(bf16[2,128,1024]{2,1,0:T(8,128)(2,1)} %pad_maximum_fusion.1), channel_id=1, source_target_pairs={{0,1},{1,0},{2,3},{3,2},{4,5},{5,4},{6,7},{7,6},{8,9},{9,8},{10,11... | collective-permute-start | bytes 1572872 | tf_op jit(solution)/shard_map/ppermute | solution.py:198
  108.6 5.6 %attn_query_side.1 = bf16[512,128]{1,0:T(8,128)(2,1)S(1)} custom-call(bf16[512,128]{1,0:T(8,128)(2,1)S(1)} %convolution_convert_fusion.6.refs_0_.q_ref, bf16[512,128]{1,0:T(8,128)(2,1)S(1)} %convolution_convert_fusion.5.refs_4_.g_ref, f32[2,512,128]{2,1,0:T(8,128)S(1)} %copy-done.9, bf16[512,256]{1,0:T(8,128)(2,1)S(1)} %convolution_convert_fusion.3.refs_1_.refs_0_.kv_ref, ...), custom_call_target="tpu_custom_call" | custom-call | flops 6442450944 | bytes 1048576 | tf_op jit(solution)/shard_map/attn_query_side/pallas_call | solution.py:179
  114.7 0.9 pad_maximum_fusion.2
  115.6 14.4 %all-to-all-start.2 = ((bf16[64,32,128]{2,1,0:T(8,128)(2,1)}), bf16[64,32,128]{2,1,0:T(8,128)(2,1)}, u32[]{:S(2)}, u32[]{:S(2)}) async-start(bf16[64,32,128]{2,1,0:T(8,128)(2,1)} %pad_maximum_fusion.2), calls=%async_computation.2 | async-start | bytes 1048576 | tf_op jit(solution)/shard_map/all_to_all | solution.py:217
  130.1 1.1 convert_element_type.69
  131.2 1.1 fusion.12
  132.7 4.7 %attn_key_side.1.refs_3_ = f32[2,512,128]{2,1,0:T(8,128)S(1)} custom-call(s32[6]{0:T(128)S(1)} %copy-done.4, bf16[512,256]{1,0:T(8,128)(2,1)S(1)} %convolution_convert_fusion.3.refs_1_.refs_0_.kv_ref, f32[8,2,512]{2,1,0:T(2,128)S(1)} %fusion.23.stat_ref, bf16[512,256]{1,0:T(8,128)(2,1)S(1)} %pad_maximum_fusion.4.refs_0_, ...), custom_call_target="tpu_custom_call" | custom-call | flops 6442450944 | bytes 1048576 | tf_op jit(solution)/shard_map/attn_key_side/pallas_call | solution.py:179
  137.4 6.7 %collective-permute-done.15 = bf16[128,1024]{1,0:T(8,128)(2,1)S(1)} collective-permute-done((bf16[128,1024]{1,0:T(8,128)(2,1)S(1)}, bf16[128,1024]{1,0:T(8,128)(2,1)S(1)}, u32[]{:S(2)}, u32[]{:S(2)}) %collective-permute-start.15) | collective-permute-done | bytes 262176 | tf_op jit(solution)/shard_map/ppermute | solution.py:198
  144.2 1.9 fusion.16
  146.0 2.2 %all-to-all-done.2 = bf16[64,32,128]{2,1,0:T(8,128)(2,1)} async-done(((bf16[64,32,128]{2,1,0:T(8,128)(2,1)}), bf16[64,32,128]{2,1,0:T(8,128)(2,1)}, u32[]{:S(2)}, u32[]{:S(2)}) %all-to-all-start.2) | async-done | bytes 524320 | tf_op jit(solution)/shard_map/all_to_all | solution.py:217
  148.3 1.1 convert_reduce_fusion.1
  149.4 2.5 %attn_key_side_end.1 = bf16[512,256]{1,0:T(8,128)(2,1)S(1)} custom-call(s32[2]{0:T(128)S(1)} %copy-done.3, bf16[512,256]{1,0:T(8,128)(2,1)S(1)} %convolution_convert_fusion.3.refs_1_.refs_0_.kv_ref, f32[8,2,512]{2,1,0:T(2,128)S(1)} %fusion.23.stat_ref, bf16[512,256]{1,0:T(8,128)(2,1)} %collective-permute-done.18.refs_0_, ...), custom_call_target="tpu_custom_call" | custom-call | flops 2147483648 | bytes 1048576 | tf_op jit(solution)/shard_map/attn_key_side_end/pallas_call | solution.py:179
  152.0 1.3 convolution_convert_fusion
  153.3 9.9 %all-to-all-start.3 = ((bf16[64,16,256]{2,1,0:T(8,128)(2,1)}), bf16[64,16,256]{2,1,0:T(8,128)(2,1)}, u32[]{:S(2)}, u32[]{:S(2)}) async-start(bf16[64,16,256]{2,1,0:T(8,128)(2,1)} %bitcast.14), calls=%async_computation.3 | async-start | bytes 1048576 | tf_op jit(solution)/shard_map/all_to_all | solution.py:217
  163.1 1.9 fusion.40
  165.1 1.4 collective-permute-start.23
  166.5 1.5 collective-permute-done.23
  169.7 5.2 %collective-permute-start.25 = (f32[16,128]{1,0:T(8,128)S(1)}, f32[16,128]{1,0:T(8,128)S(1)}, u32[]{:S(2)}, u32[]{:S(2)}) collective-permute-start(f32[16,128]{1,0:T(8,128)S(1)} %get-tuple-element.27), channel_id=1, source_target_pairs={{0,0},{1,64},{2,128},{3,192},{32,1},{33,65},{34,129},{35,193},{64,... | collective-permute-start | bytes 24584 | tf_op jit(solution)/shard_map/ppermute | solution.py:376
  176.2 4.2 %all-to-all-done.3 = bf16[64,16,256]{2,1,0:T(8,128)(2,1)} async-done(((bf16[64,16,256]{2,1,0:T(8,128)(2,1)}), bf16[64,16,256]{2,1,0:T(8,128)(2,1)}, u32[]{:S(2)}, u32[]{:S(2)}) %all-to-all-start.3) | async-done | bytes 524320 | tf_op jit(solution)/shard_map/all_to_all | solution.py:217
  180.4 1.1 convert_reduce_fusion
  181.6 1.3 pad_maximum_fusion.6
  182.9 1.4 reshape.286
  184.2 7.2 %all-to-all-start.4 = ((f32[4,4,384]{2,1,0:T(4,128)}), f32[4,4,384]{2,1,0:T(4,128)}, u32[]{:S(2)}, u32[]{:S(2)}) async-start(f32[4,4,384]{2,1,0:T(4,128)} %reshape.286), calls=%async_computation.4 | async-start | bytes 49152 | tf_op jit(solution)/shard_map/all_to_all | solution.py:217
  191.5 1.8 fusion.21
  193.3 1.5 all-to-all-done.4
  194.7 1.3 slice_bitcast_fusion.9
  (118 shorter events, 12.9 us)
Async XLA Ops:
  0.6 3.5 %copy-start = (bf16[64,1024]{1,0:T(8,128)(2,1)S(1)}, bf16[64,1024]{1,0:T(8,128)(2,1)}, u32[]{:S(2)}) copy-start(bf16[64,1024]{1,0:T(8,128)(2,1)} %param.20) | copy-start | bytes 393220
  0.6 19.2 %copy-start.19 = (bf16[1,128,1024]{2,1,0:T(8,128)(2,1)S(1)}, bf16[1,128,1024]{2,1,0:T(8,128)(2,1)}, u32[]{:S(2)}) copy-start(bf16[1,128,1024]{2,1,0:T(8,128)(2,1)} %param.15) | copy-start | bytes 786436
  0.7 10.2 %collective-permute-start.1 = (bf16[128,1024]{1,0:T(8,128)(2,1)}, bf16[128,1024]{1,0:T(8,128)(2,1)S(1)}, u32[]{:S(2)}, u32[]{:S(2)}) collective-permute-start(bf16[128,1024]{1,0:T(8,128)(2,1)} %bitcast.97), channel_id=1, source_target_pairs={{0,2},{1,3},{2,0},{3,1},{4,6},{5,7},{6,4},{7,5},{8,10},{9,11},{10,... | collective-permute-start | bytes 786440 | tf_op jit(solution)/shard_map/ppermute | solution.py:198
  2.8 17.1 %collective-permute-start = (bf16[128,1024]{1,0:T(8,128)(2,1)}, bf16[128,1024]{1,0:T(8,128)(2,1)S(1)}, u32[]{:S(2)}, u32[]{:S(2)}) collective-permute-start(bf16[128,1024]{1,0:T(8,128)(2,1)} %bitcast.98), channel_id=1, source_target_pairs={{0,1},{1,0},{2,3},{3,2},{4,5},{5,4},{6,7},{7,6},{8,9},{9,8},{10,11... | collective-permute-start | bytes 786440 | tf_op jit(solution)/shard_map/ppermute | solution.py:198
  4.1 6.7 %collective-permute-start.3 = (bf16[16,1024]{1,0:T(8,128)(2,1)S(1)}, bf16[16,1024]{1,0:T(8,128)(2,1)S(1)}, u32[]{:S(2)}, u32[]{:S(2)}) collective-permute-start(bf16[16,1024]{1,0:T(8,128)(2,1)S(1)} %constant_dynamic-slice_fusion.1), channel_id=1, source_target_pairs={{0,0},{1,32},{2,64},{3,96},{32,128},{33,160},{34,192},{35,224},{64... | collective-permute-start | bytes 98312 | tf_op jit(solution)/shard_map/ppermute | solution.py:259
  10.9 9.0 %collective-permute-start.2 = (bf16[128,1024]{1,0:T(8,128)(2,1)S(1)}, bf16[128,1024]{1,0:T(8,128)(2,1)}, u32[]{:S(2)}, u32[]{:S(2)}) collective-permute-start(bf16[128,1024]{1,0:T(8,128)(2,1)S(1)} %collective-permute-done.1), channel_id=1, source_target_pairs={{0,1},{1,0},{2,3},{3,2},{4,5},{5,4},{6,7},{7,6},{8,9},{9,8},{10,11... | collective-permute-start | bytes 786440 | tf_op jit(solution)/shard_map/ppermute | solution.py:198
  12.1 8.8 %copy-start.16 = (bf16[1,128,1024]{2,1,0:T(8,128)(2,1)S(1)}, bf16[1,128,1024]{2,1,0:T(8,128)(2,1)}, u32[]{:S(2)}) copy-start(bf16[1,128,1024]{2,1,0:T(8,128)(2,1)} %param.16) | copy-start | bytes 786436
  12.1 9.2 %copy-start.21 = (s32[32,32]{1,0:T(8,128)S(1)}, s32[32,32]{1,0:T(8,128)}, u32[]{:S(2)}) copy-start(s32[32,32]{1,0:T(8,128)} %param.21) | copy-start | bytes 12292
  12.1 28.6 %all-to-all-start = ((bf16[8,128,512]{2,1,0:T(8,128)(2,1)}), bf16[8,128,512]{2,1,0:T(8,128)(2,1)S(1)}, u32[]{:S(2)}, u32[]{:S(2)}) async-start(bf16[8,128,512]{2,1,0:T(8,128)(2,1)} %broadcast_in_dim.41), calls=%async_computation | async-start | bytes 2097152 | tf_op jit(solution)/shard_map/all_to_all | solution.py:217
  20.9 28.0 %copy-start.10 = (bf16[512,1024]{1,0:T(8,128)(2,1)}, bf16[512,1024]{1,0:T(8,128)(2,1)S(1)}, u32[]{:S(2)}) copy-start(bf16[512,1024]{1,0:T(8,128)(2,1)S(1)} %pad_maximum_fusion) | copy-start | bytes 3145732
  20.9 17.4 %collective-permute-start.11 = (bf16[128,1024]{1,0:T(8,128)(2,1)S(1)}, bf16[128,1024]{1,0:T(8,128)(2,1)S(1)}, u32[]{:S(2)}, u32[]{:S(2)}) collective-permute-start(bf16[128,1024]{1,0:T(8,128)(2,1)S(1)} %bitcast.94), channel_id=1, source_target_pairs={{0,1},{1,0},{2,3},{3,2},{4,5},{5,4},{6,7},{7,6},{8,9},{9,8},{10,11... | collective-permute-start | bytes 786440 | tf_op jit(solution)/shard_map/ppermute | solution.py:198
  21.3 16.2 %collective-permute-start.12 = (bf16[128,1024]{1,0:T(8,128)(2,1)S(1)}, bf16[128,1024]{1,0:T(8,128)(2,1)}, u32[]{:S(2)}, u32[]{:S(2)}) collective-permute-start(bf16[128,1024]{1,0:T(8,128)(2,1)S(1)} %bitcast.95), channel_id=1, source_target_pairs={{0,2},{1,3},{2,0},{3,1},{4,6},{5,7},{6,4},{7,5},{8,10},{9,11},{10,... | collective-permute-start | bytes 786440 | tf_op jit(solution)/shard_map/ppermute | solution.py:198
  37.5 12.9 %collective-permute-start.13 = (bf16[128,1024]{1,0:T(8,128)(2,1)}, bf16[128,1024]{1,0:T(8,128)(2,1)}, u32[]{:S(2)}, u32[]{:S(2)}) collective-permute-start(bf16[128,1024]{1,0:T(8,128)(2,1)} %collective-permute-done.12), channel_id=1, source_target_pairs={{0,1},{1,0},{2,3},{3,2},{4,5},{5,4},{6,7},{7,6},{8,9},{9,8},{10,11... | collective-permute-start | bytes 786440 | tf_op jit(solution)/shard_map/ppermute | solution.py:198
  40.7 1.0 copy-start.13
  42.2 14.4 %collective-permute-start.4 = (bf16[512,256]{1,0:T(8,128)(2,1)S(1)}, bf16[512,256]{1,0:T(8,128)(2,1)S(1)}, u32[]{:S(2)}, u32[]{:S(2)}) collective-permute-start(bf16[512,256]{1,0:T(8,128)(2,1)S(1)} %convolution_convert_fusion.3.refs_1_.refs_0_.kv_ref), channel_id=1, source_target_pairs={{4,0},{8,4},{12,8},{16,12},{20,16},{24,20},{28,24},{0,28},{5,1},{9... | collective-permute-start | bytes 786440 | tf_op jit(solution)/shard_map/ppermute | solution.py:194
  47.8 11.4 %collective-permute-start.8 = (bf16[512,256]{1,0:T(8,128)(2,1)S(1)}, bf16[512,256]{1,0:T(8,128)(2,1)S(1)}, u32[]{:S(2)}, u32[]{:S(2)}) collective-permute-start(bf16[512,256]{1,0:T(8,128)(2,1)S(1)} %convolution_convert_fusion.3.refs_1_.refs_0_.kv_ref), channel_id=1, source_target_pairs={{28,0},{0,4},{4,8},{8,12},{12,16},{16,20},{20,24},{24,28},{29,1},{... | collective-permute-start | bytes 786440 | tf_op jit(solution)/shard_map/ppermute | solution.py:194
  48.9 16.2 %copy-start.14 = (bf16[128,1024]{1,0:T(8,128)(2,1)}, bf16[128,1024]{1,0:T(8,128)(2,1)S(1)}, u32[]{:S(2)}) copy-start(bf16[128,1024]{1,0:T(8,128)(2,1)S(1)} %reshape.267) | copy-start | bytes 786436
  53.8 28.3 %copy-start.7 = (s32[2]{0:T(128)S(1)}, s32[2]{0:T(128)}, u32[]{:S(2)}) copy-start(s32[2]{0:T(128)} %constant.137.clone.number_ref) | copy-start | bytes 28
  53.8 7.9 %collective-permute-start.19 = (bf16[512,256]{1,0:T(8,128)(2,1)S(1)}, bf16[512,256]{1,0:T(8,128)(2,1)S(1)}, u32[]{:S(2)}, u32[]{:S(2)}) collective-permute-start(bf16[512,256]{1,0:T(8,128)(2,1)S(1)} %pad_maximum_fusion.4.refs_0_), channel_id=1, source_target_pairs={{4,0},{8,4},{12,8},{16,12},{20,16},{24,20},{28,24},{0,28},{5,1},{9... | collective-permute-start | bytes 786440 | tf_op jit(solution)/shard_map/ppermute | solution.py:194
  56.6 8.5 %collective-permute-start.16 = (bf16[512,256]{1,0:T(8,128)(2,1)S(1)}, bf16[512,256]{1,0:T(8,128)(2,1)S(1)}, u32[]{:S(2)}, u32[]{:S(2)}) collective-permute-start(bf16[512,256]{1,0:T(8,128)(2,1)S(1)} %pad_maximum_fusion.4.refs_0_), channel_id=1, source_target_pairs={{28,0},{0,4},{4,8},{8,12},{12,16},{16,20},{20,24},{24,28},{29,1},{... | collective-permute-start | bytes 786440 | tf_op jit(solution)/shard_map/ppermute | solution.py:194
  56.6 10.7 %collective-permute-start.5 = (bf16[512,256]{1,0:T(8,128)(2,1)S(1)}, bf16[512,256]{1,0:T(8,128)(2,1)S(1)}, u32[]{:S(2)}, u32[]{:S(2)}) collective-permute-start(bf16[512,256]{1,0:T(8,128)(2,1)S(1)} %collective-permute-done.4.refs_1_), channel_id=1, source_target_pairs={{4,0},{8,4},{12,8},{16,12},{20,16},{24,20},{28,24},{0,28},{5,1},{9... | collective-permute-start | bytes 786440 | tf_op jit(solution)/shard_map/ppermute | solution.py:194
  59.3 11.5 %collective-permute-start.9 = (bf16[512,256]{1,0:T(8,128)(2,1)S(1)}, bf16[512,256]{1,0:T(8,128)(2,1)}, u32[]{:S(2)}, u32[]{:S(2)}) collective-permute-start(bf16[512,256]{1,0:T(8,128)(2,1)S(1)} %collective-permute-done.8.refs_2_.refs_7_), channel_id=1, source_target_pairs={{28,0},{0,4},{4,8},{8,12},{12,16},{16,20},{20,24},{24,28},{29,1},{... | collective-permute-start | bytes 786440 | tf_op jit(solution)/shard_map/ppermute | solution.py:194
  61.7 11.2 %collective-permute-start.20 = (bf16[512,256]{1,0:T(8,128)(2,1)S(1)}, bf16[512,256]{1,0:T(8,128)(2,1)S(1)}, u32[]{:S(2)}, u32[]{:S(2)}) collective-permute-start(bf16[512,256]{1,0:T(8,128)(2,1)S(1)} %collective-permute-done.19.refs_1_), channel_id=1, source_target_pairs={{4,0},{8,4},{12,8},{16,12},{20,16},{24,20},{28,24},{0,28},{5,1},{9... | collective-permute-start | bytes 786440 | tf_op jit(solution)/shard_map/ppermute | solution.py:194
  65.1 20.6 %collective-permute-start.17 = (bf16[512,256]{1,0:T(8,128)(2,1)S(1)}, bf16[512,256]{1,0:T(8,128)(2,1)S(1)}, u32[]{:S(2)}, u32[]{:S(2)}) collective-permute-start(bf16[512,256]{1,0:T(8,128)(2,1)S(1)} %collective-permute-done.16.refs_2_), channel_id=1, source_target_pairs={{28,0},{0,4},{4,8},{8,12},{12,16},{16,20},{20,24},{24,28},{29,1},{... | collective-permute-start | bytes 786440 | tf_op jit(solution)/shard_map/ppermute | solution.py:194
  67.3 11.2 %collective-permute-start.6 = (bf16[512,256]{1,0:T(8,128)(2,1)S(1)}, bf16[512,256]{1,0:T(8,128)(2,1)}, u32[]{:S(2)}, u32[]{:S(2)}) collective-permute-start(bf16[512,256]{1,0:T(8,128)(2,1)S(1)} %collective-permute-done.5.refs_1_.refs_2_), channel_id=1, source_target_pairs={{4,0},{8,4},{12,8},{16,12},{20,16},{24,20},{28,24},{0,28},{5,1},{9... | collective-permute-start | bytes 786440 | tf_op jit(solution)/shard_map/ppermute | solution.py:194
  70.7 15.1 %collective-permute-start.10 = (bf16[512,256]{1,0:T(8,128)(2,1)}, bf16[512,256]{1,0:T(8,128)(2,1)}, u32[]{:S(2)}, u32[]{:S(2)}) collective-permute-start(bf16[512,256]{1,0:T(8,128)(2,1)} %collective-permute-done.9.refs_2_.refs_6_), channel_id=1, source_target_pairs={{28,0},{0,4},{4,8},{8,12},{12,16},{16,20},{20,24},{24,28},{29,1},{... | collective-permute-start | bytes 786440 | tf_op jit(solution)/shard_map/ppermute | solution.py:194
  72.2 11.4 %copy-start.6 = (s32[2]{0:T(128)S(1)}, s32[2]{0:T(128)}, u32[]{:S(2)}) copy-start(s32[2]{0:T(128)} %constant.138.clone.number_ref) | copy-start | bytes 28
  72.9 15.0 %collective-permute-start.21 = (bf16[512,256]{1,0:T(8,128)(2,1)S(1)}, bf16[512,256]{1,0:T(8,128)(2,1)S(1)}, u32[]{:S(2)}, u32[]{:S(2)}) collective-permute-start(bf16[512,256]{1,0:T(8,128)(2,1)S(1)} %collective-permute-done.20.refs_3_), channel_id=1, source_target_pairs={{4,0},{8,4},{12,8},{16,12},{20,16},{24,20},{28,24},{0,28},{5,1},{9... | collective-permute-start | bytes 786440 | tf_op jit(solution)/shard_map/ppermute | solution.py:194
  78.5 12.1 %collective-permute-start.7 = (bf16[512,256]{1,0:T(8,128)(2,1)}, bf16[512,256]{1,0:T(8,128)(2,1)S(1)}, u32[]{:S(2)}, u32[]{:S(2)}) collective-permute-start(bf16[512,256]{1,0:T(8,128)(2,1)} %collective-permute-done.6.refs_1_.refs_3_), channel_id=1, source_target_pairs={{4,0},{8,4},{12,8},{16,12},{20,16},{24,20},{28,24},{0,28},{5,1},{9... | collective-permute-start | bytes 786440 | tf_op jit(solution)/shard_map/ppermute | solution.py:194
  83.7 2.1 %copy-start.5 = (s32[2]{0:T(128)S(1)}, s32[2]{0:T(128)}, u32[]{:S(2)}) copy-start(s32[2]{0:T(128)} %constant.139.clone.number_ref) | copy-start | bytes 28
  85.7 7.4 %copy-start.15 = (bf16[128,1024]{1,0:T(8,128)(2,1)S(1)}, bf16[128,1024]{1,0:T(8,128)(2,1)}, u32[]{:S(2)}) copy-start(bf16[128,1024]{1,0:T(8,128)(2,1)} %copy-done.14) | copy-start | bytes 786436
  85.7 63.7 %collective-permute-start.18 = (bf16[512,256]{1,0:T(8,128)(2,1)S(1)}, bf16[512,256]{1,0:T(8,128)(2,1)}, u32[]{:S(2)}, u32[]{:S(2)}) collective-permute-start(bf16[512,256]{1,0:T(8,128)(2,1)S(1)} %collective-permute-done.17.refs_4_), channel_id=1, source_target_pairs={{28,0},{0,4},{4,8},{8,12},{12,16},{16,20},{20,24},{24,28},{29,1},{... | collective-permute-start | bytes 786440 | tf_op jit(solution)/shard_map/ppermute | solution.py:194
  87.9 61.5 %collective-permute-start.22 = (bf16[512,256]{1,0:T(8,128)(2,1)S(1)}, bf16[512,256]{1,0:T(8,128)(2,1)}, u32[]{:S(2)}, u32[]{:S(2)}) collective-permute-start(bf16[512,256]{1,0:T(8,128)(2,1)S(1)} %collective-permute-done.21.refs_5_), channel_id=1, source_target_pairs={{4,0},{8,4},{12,8},{16,12},{20,16},{24,20},{28,24},{0,28},{5,1},{9... | collective-permute-start | bytes 786440 | tf_op jit(solution)/shard_map/ppermute | solution.py:194
  91.6 0.7 copy-start.1
  92.3 0.8 copy-start.8
  100.0 15.6 %all-to-all-start.1 = ((f32[8,1,8,128]{3,2,1,0:T(8,128)}), f32[8,1,8,128]{3,2,1,0:T(8,128)S(1)}, u32[]{:S(2)}, u32[]{:S(2)}) async-start(f32[8,1,8,128]{3,2,1,0:T(8,128)} %broadcast_in_dim.48), calls=%async_computation.1 | async-start | bytes 65536 | tf_op jit(solution)/shard_map/all_to_all | solution.py:217
  103.8 4.8 %copy-start.2 = (bf16[512,256]{1,0:T(8,128)(2,1)S(1)}, bf16[512,256]{1,0:T(8,128)(2,1)}, u32[]{:S(2)}) copy-start(bf16[512,256]{1,0:T(8,128)(2,1)} %copy-done.1) | copy-start | bytes 786436
  103.8 4.8 %copy-start.9 = (f32[2,512,128]{2,1,0:T(8,128)S(1)}, f32[2,512,128]{2,1,0:T(8,128)}, u32[]{:S(2)}) copy-start(f32[2,512,128]{2,1,0:T(8,128)} %copy-done.8) | copy-start | bytes 1572868
  105.8 24.2 %collective-permute-start.14 = (bf16[2,128,1024]{2,1,0:T(8,128)(2,1)}, bf16[2,128,1024]{2,1,0:T(8,128)(2,1)}, u32[]{:S(2)}, u32[]{:S(2)}) collective-permute-start(bf16[2,128,1024]{2,1,0:T(8,128)(2,1)} %pad_maximum_fusion.1), channel_id=1, source_target_pairs={{0,1},{1,0},{2,3},{3,2},{4,5},{5,4},{6,7},{7,6},{8,9},{9,8},{10,11... | collective-permute-start | bytes 1572872 | tf_op jit(solution)/shard_map/ppermute | solution.py:198
  108.6 5.6 %copy-start.11 = (bf16[512,1024]{1,0:T(8,128)(2,1)S(1)}, bf16[512,1024]{1,0:T(8,128)(2,1)}, u32[]{:S(2)}) copy-start(bf16[512,1024]{1,0:T(8,128)(2,1)} %copy-done.10) | copy-start | bytes 3145732
  108.6 6.1 %copy-start.18 = (bf16[64,16,128]{2,1,0:T(8,128)(2,1)S(1)}, bf16[64,16,128]{2,1,0:T(8,128)(2,1)}, u32[]{:S(2)}) copy-start(bf16[64,16,128]{2,1,0:T(8,128)(2,1)} %reshape.280) | copy-start | bytes 786436
  115.6 17.2 %copy-start.4 = (s32[6]{0:T(128)S(1)}, s32[6]{0:T(128)}, u32[]{:S(2)}) copy-start(s32[6]{0:T(128)} %constant.141.clone.number_ref) | copy-start | bytes 76
  115.6 32.7 %all-to-all-start.2 = ((bf16[64,32,128]{2,1,0:T(8,128)(2,1)}), bf16[64,32,128]{2,1,0:T(8,128)(2,1)}, u32[]{:S(2)}, u32[]{:S(2)}) async-start(bf16[64,32,128]{2,1,0:T(8,128)(2,1)} %pad_maximum_fusion.2), calls=%async_computation.2 | async-start | bytes 1048576 | tf_op jit(solution)/shard_map/all_to_all | solution.py:217
  132.3 11.8 %copy-start.20 = (bf16[1,128,1024]{2,1,0:T(8,128)(2,1)S(1)}, bf16[1,128,1024]{2,1,0:T(8,128)(2,1)}, u32[]{:S(2)}) copy-start(bf16[1,128,1024]{2,1,0:T(8,128)(2,1)} %param.15) | copy-start | bytes 786436
  132.3 11.8 %collective-permute-start.15 = (bf16[128,1024]{1,0:T(8,128)(2,1)S(1)}, bf16[128,1024]{1,0:T(8,128)(2,1)S(1)}, u32[]{:S(2)}, u32[]{:S(2)}) collective-permute-start(bf16[128,1024]{1,0:T(8,128)(2,1)S(1)} %fusion.12), channel_id=1, source_target_pairs={{0,2},{1,3},{2,0},{3,1},{4,6},{5,7},{6,4},{7,5},{8,10},{9,11},{10,... | collective-permute-start | bytes 786440 | tf_op jit(solution)/shard_map/ppermute | solution.py:198
  137.4 12.0 %copy-start.3 = (s32[2]{0:T(128)S(1)}, s32[2]{0:T(128)}, u32[]{:S(2)}) copy-start(s32[2]{0:T(128)} %constant.142.clone.number_ref) | copy-start | bytes 28
  149.4 2.6 %copy-start.12 = (bf16[512,1024]{1,0:T(8,128)(2,1)S(1)}, bf16[512,1024]{1,0:T(8,128)(2,1)}, u32[]{:S(2)}) copy-start(bf16[512,1024]{1,0:T(8,128)(2,1)} %copy-done.10) | copy-start | bytes 3145732
  153.3 27.1 %all-to-all-start.3 = ((bf16[64,16,256]{2,1,0:T(8,128)(2,1)}), bf16[64,16,256]{2,1,0:T(8,128)(2,1)}, u32[]{:S(2)}, u32[]{:S(2)}) async-start(bf16[64,16,256]{2,1,0:T(8,128)(2,1)} %bitcast.14), calls=%async_computation.3 | async-start | bytes 1048576 | tf_op jit(solution)/shard_map/all_to_all | solution.py:217
  165.1 26.4 %copy-start.17 = (bf16[1,128,1024]{2,1,0:T(8,128)(2,1)S(1)}, bf16[1,128,1024]{2,1,0:T(8,128)(2,1)}, u32[]{:S(2)}) copy-start(bf16[1,128,1024]{2,1,0:T(8,128)(2,1)} %param.16) | copy-start | bytes 786436
  165.1 2.9 %collective-permute-start.23 = (bf16[2,128,1024]{2,1,0:T(8,128)(2,1)S(1)}, bf16[2,128,1024]{2,1,0:T(8,128)(2,1)S(1)}, u32[]{:S(2)}, u32[]{:S(2)}) collective-permute-start(bf16[2,128,1024]{2,1,0:T(8,128)(2,1)S(1)} %pad_maximum_fusion.3), channel_id=1, source_target_pairs={{0,1},{1,0},{2,3},{3,2},{4,5},{5,4},{6,7},{7,6},{8,9},{9,8},{10,11... | collective-permute-start | bytes 1572872 | tf_op jit(solution)/shard_map/ppermute | solution.py:198
  168.9 22.5 %collective-permute-start.24 = (bf16[128,1024]{1,0:T(8,128)(2,1)}, bf16[128,1024]{1,0:T(8,128)(2,1)}, u32[]{:S(2)}, u32[]{:S(2)}) collective-permute-start(bf16[128,1024]{1,0:T(8,128)(2,1)} %fusion.6), channel_id=1, source_target_pairs={{0,2},{1,3},{2,0},{3,1},{4,6},{5,7},{6,4},{7,5},{8,10},{9,11},{10,... | collective-permute-start | bytes 786440 | tf_op jit(solution)/shard_map/ppermute | solution.py:198
  169.7 5.9 %collective-permute-start.25 = (f32[16,128]{1,0:T(8,128)S(1)}, f32[16,128]{1,0:T(8,128)S(1)}, u32[]{:S(2)}, u32[]{:S(2)}) collective-permute-start(f32[16,128]{1,0:T(8,128)S(1)} %get-tuple-element.27), channel_id=1, source_target_pairs={{0,0},{1,64},{2,128},{3,192},{32,1},{33,65},{34,129},{35,193},{64,... | collective-permute-start | bytes 24584 | tf_op jit(solution)/shard_map/ppermute | solution.py:376
  184.2 10.5 %all-to-all-start.4 = ((f32[4,4,384]{2,1,0:T(4,128)}), f32[4,4,384]{2,1,0:T(4,128)}, u32[]{:S(2)}, u32[]{:S(2)}) async-start(f32[4,4,384]{2,1,0:T(4,128)} %reshape.286), calls=%async_computation.4 | async-start | bytes 49152 | tf_op jit(solution)/shard_map/all_to_all | solution.py:217
